TPU v7x, 256 devices: a whole 4x4x8 slice. The times are simulated.
256 devices in a mesh: member: 8 (over x, core), lat: 32 (over z, y).
Axes of the slice: x: 4, y: 4, z: 8, core: 2. Of those that a mesh axis runs over, the one named last changes fastest.
Arguments:
- velocity: bfloat16 [16, 8, 1024, 2048], P('member', None, 'lat'), may hold values from -6 to 6
- tracer: bfloat16 [16, 8, 1024, 2048], P('member', None, 'lat'), may hold values from -6 to 6
- wave_slots: int32 [768], replicated, may hold values from 0 to 767, each once
- parents: int32 [16], replicated, may hold values from 0 to 15, as said below
- noise: bfloat16 [768, 16, 2, 8, 683], P('lat', 'member'), may hold values from -4 to 4
Outputs:
- child_spectra: bfloat16 [768, 16, 2, 8, 683], P('lat', 'member')
- child_fourier: bfloat16 [768, 16, 2, 8, 1024], P('lat', 'member')
Inputs may be any that keep to these rules, and one draw needn't show every extreme that they name: `wave_slots`: each number below 683 stands in exactly one slot; a slot holding 683 or more is empty. `parents`: the parent of child i lies within 2 of i, and some child's parent is exactly 2 above it.
All inputs are finite; a program needn't handle non-finite values.
Results may differ from a plain program's by a relative error of at most 0.008.
Values may be sent and summed in bfloat16 or wider, within the bound.
A program may use at most 64 MiB of HBM per device.

v0:
```python
import math

import jax
import jax.numpy as jnp
from jax import lax
from jax.sharding import PartitionSpec as P

NLAT = 1024
NLON = 2048
TRUNC = 683
SPREAD = 2


def extended(block, sides, width):
    for axis, dim in sides:
        count = lax.axis_size(axis)
        forward = [(i, i + 1) for i in range(count - 1)]
        backward = [(target, source) for source, target in forward]
        low = lax.ppermute(
            lax.slice_in_dim(block, block.shape[dim] - width, None, axis=dim), axis, forward
        )
        high = lax.ppermute(lax.slice_in_dim(block, 0, width, axis=dim), axis, backward)
        block = jnp.concatenate([low, block, high], axis=dim)
    return block


def zonal_table(wavenumbers):
    longitude = jnp.arange(NLON, dtype=jnp.int32)
    active = (wavenumbers < TRUNC).astype(jnp.float32)
    phase = wavenumbers[:, None] * longitude[None, :] % NLON
    angle = phase.astype(jnp.float32) * (2.0 * math.pi / NLON)
    weight = active[:, None] / math.sqrt(NLON)
    table = jnp.stack([jnp.cos(angle) * weight, -jnp.sin(angle) * weight], axis=1)
    return table.astype(jnp.bfloat16)


def meridional_table(wavenumbers):
    degree = jnp.arange(TRUNC, dtype=jnp.int32)
    latitude = jnp.arange(NLAT, dtype=jnp.int32)
    phase = degree[:, None] * (2 * latitude + 1)[None, :] % (4 * NLAT)
    angle = phase.astype(jnp.float32) * (math.pi / (2 * NLAT))
    factor = math.sqrt(2.0 / NLAT)
    even_table = (jnp.cos(angle) * factor).astype(jnp.bfloat16)
    odd_table = (jnp.sin(angle) * factor).astype(jnp.bfloat16)
    active = (degree[None, :] >= wavenumbers[:, None]) & (wavenumbers[:, None] < TRUNC)
    is_odd = (wavenumbers % 2 == 1)[:, None, None]
    table = jnp.where(is_odd, odd_table[None], even_table[None])
    return jnp.where(active[:, :, None], table, jnp.zeros((), jnp.bfloat16))


def per_device(velocity, tracer, wave_slots, parents, noise):
    lat_count = lax.axis_size("lat")
    lat_index = lax.axis_index("lat")
    group_index = lax.axis_index("member")
    mem_local, field_count, lat_local, lon_count = velocity.shape
    slots_all = wave_slots.shape[0]
    slots_here = slots_all // lat_count
    product = (velocity.astype(jnp.float32) * tracer.astype(jnp.float32)).astype(jnp.bfloat16)
    table = zonal_table(wave_slots)
    fourier = jnp.einsum(
        "sck,mflk->smcfl", table, product, preferred_element_type=jnp.float32
    ).astype(jnp.bfloat16)
    outgoing = fourier.reshape(slots_all, 1, mem_local * 2 * field_count * lat_local)
    received = lax.all_to_all(outgoing, "lat", split_axis=0, concat_axis=1, tiled=True)
    received = received.reshape(slots_here, lat_count, mem_local, 2, field_count, lat_local)
    own_waves = lax.dynamic_slice_in_dim(wave_slots, lat_index * slots_here, slots_here)
    basis = meridional_table(own_waves)
    basis_split = basis.reshape(slots_here, TRUNC, lat_count, lat_local)
    first_member = group_index * mem_local

    def forward(coefficients):
        return jnp.einsum(
            "sgmcfl,sngl->smcfn", coefficients, basis_split, preferred_element_type=jnp.float32
        ).astype(jnp.bfloat16)

    spectra = forward(received)
    spectra_wide = extended(spectra, (("member", 1),), SPREAD)
    own_parents = lax.dynamic_slice_in_dim(parents, first_member, mem_local)
    offset = own_parents - first_member + SPREAD
    columns = jnp.arange(mem_local + 2 * SPREAD, dtype=jnp.int32)
    selector = (offset[:, None] == columns[None, :]).astype(jnp.bfloat16)
    chosen = jnp.einsum(
        "ip,spcfn->sicfn", selector, spectra_wide, preferred_element_type=jnp.float32
    )
    degree = jnp.arange(TRUNC, dtype=jnp.int32)
    active = ((degree[None, :] >= own_waves[:, None]) & (own_waves[:, None] < TRUNC)).astype(
        jnp.float32
    )
    children = (chosen + noise.astype(jnp.float32) * active[:, None, None, None, :]).astype(
        jnp.bfloat16
    )
    returned = jnp.einsum(
        "sicfn,snj->sicfj", children, basis, preferred_element_type=jnp.float32
    ).astype(jnp.bfloat16)
    return (children, returned)


def solution(mesh):
    in_specs = (
        P("member", None, "lat", None),
        P("member", None, "lat", None),
        P(),
        P(),
        P("lat", "member", None, None, None),
    )
    out_specs = (P("lat", "member", None, None, None), P("lat", "member", None, None, None))
    return jax.shard_map(
        per_device, mesh=mesh, in_specs=in_specs, out_specs=out_specs, check_vma=False
    )
```

profile of v0, /device:TPU:1, one launch (start us, length us, event | category | flops | bytes accessed | tf_op | source)
XLA Modules:
  0.0 152.8 jit_solution(4370821730776843014)
XLA Ops:
  0.6 0.7 compare_select_fusion
  1.3 28.0 %multiply_convert_fusion.1 = (bf16[768,1,2048]{2,0,1:T(8,128)(2,1)S(1)}, bf16[768,1,2048]{2,0,1:T(8,128)(2,1)S(1)}) fusion(f32[768]{0:T(1024)S(1)} %compare_select_fusion, s32[768]{0:T(1024)} %param.7), kind=kLoop, calls=%fused_computation.30 | loop fusion | flops 29884416 | bytes 6297600 | tf_op jit(solution)/shard_map/convert
  29.3 0.0 copy-done.4
  29.4 0.0 copy-done.5
  29.4 3.5 %fusion.57 = bf16[768,2,2,8,32]{0,4,2,3,1:T(8,128)(2,1)S(1)} fusion(bf16[768,1,2048]{2,0,1:T(8,128)(2,1)S(1)} %get-tuple-element.13, bf16[768,1,2048]{2,0,1:T(8,128)(2,1)S(1)} %get-tuple-element.12, bf16[2,8,32,2048]{3,2,1,0:T(8,128)(2,1)S(1)} %copy-done.4, bf16[2,8,32,2048]{3,2,1,0:T(8,128)(2,1)S(1)} %copy-done.5), kind=kOutput, calls=%fused_computation.66 | convolution fusion | flops 3238789120 | bytes 12058624 | tf_op jit(solution)/shard_map/sck,mflk->smcfl/dot_general | solution.py:60
  32.8 0.1 copy.19
  32.9 0.5 broadcast.349
  33.5 1.9 %reduce = bf16[768,1024]{0,1:T(8,128)(2,1)S(1)} reduce(bf16[768,1,1024]{0,2,1:T(8,128)(2,1)S(1)} %bitcast.55, bf16[]{:T(256)} %broadcast.349), dimensions={1}, to_apply=%copy.20.reduce_sub_computation | reduce | bytes 3145730 | tf_op jit(solution)/shard_map/reshape | solution.py:63
  35.3 0.8 copy.45
  36.1 1.9 %reshape.301 = bf16[32,2,12288]{2,1,0:T(2,128)(2,1)} reshape(bf16[768,1024]{1,0:T(8,128)(2,1)S(1)} %copy.45) | data formatting | bytes 3145728
  38.0 12.3 %all-to-all-start = ((bf16[32,2,12288]{2,1,0:T(2,128)(2,1)}), bf16[32,2,12288]{2,1,0:T(2,128)(2,1)}, u32[]{:S(2)}, u32[]{:S(2)}) async-start(bf16[32,2,12288]{2,1,0:T(2,128)(2,1)} %reshape.301), calls=%async_computation | async-start | bytes 3145728 | tf_op jit(solution)/shard_map/all_to_all | solution.py:64
  50.3 0.8 broadcast_compare_fusion
  51.1 0.1 fusion.70
  51.2 15.0 %multiply_convert_fusion.4 = (bf16[683,32,32]{0,2,1:T(8,128)(2,1)}, bf16[683,32,32]{0,2,1:T(8,128)(2,1)}) fusion(s32[32,32]{1,0:T(8,128)S(1)} %multiply_add_fusion), kind=kLoop, calls=%fused_computation.48 | loop fusion | flops 12589056 | bytes 2801664 | tf_op jit(solution)/shard_map/convert_element_type | solution.py:44
  66.2 21.9 %all-to-all-done = bf16[32,2,12288]{2,1,0:T(2,128)(2,1)} async-done(((bf16[32,2,12288]{2,1,0:T(2,128)(2,1)}), bf16[32,2,12288]{2,1,0:T(2,128)(2,1)}, u32[]{:S(2)}, u32[]{:S(2)}) %all-to-all-start) | async-done | bytes 1572896 | tf_op jit(solution)/shard_map/all_to_all | solution.py:64
  88.1 8.2 %reshape.302 = bf16[768,1,1024]{2,1,0:T(2,128)(2,1)S(1)} reshape(bf16[32,2,12288]{2,1,0:T(2,128)(2,1)} %all-to-all-done) | data formatting | bytes 3145728
  96.3 1.8 %copy.35 = bf16[768,1,1024]{2,0,1:T(8,128)(2,1)} copy(bf16[768,1,1024]{2,1,0:T(2,128)(2,1)S(1)} %reshape.302) | data formatting | bytes 3145728
  98.1 8.5 %reshape.300 = bf16[24,32,2,2,8,32]{5,4,3,2,0,1:T(8,128)(2,1)} reshape(bf16[24,32,1,1024]{3,0,1,2:T(8,128)(2,1)} %bitcast.56) | data formatting | bytes 3145728 | tf_op jit(solution)/shard_map/reshape | solution.py:65
  106.6 0.0 copy-done
  106.7 10.8 %bitcast_convert_fusion = bf16[24,2,2,8,683]{4,3,2,1,0:T(8,128)(2,1)} fusion(pred[24]{0:T(512)(128)(4,1)S(1)} %fusion.64, pred[24,683]{1,0:T(8,128)(4,1)S(1)} %get-tuple-element.17, bf16[683,32,32]{0,2,1:T(8,128)(2,1)S(1)} %copy-done.1, bf16[683,32,32]{0,2,1:T(8,128)(2,1)S(1)} %copy-done, bf16[24,32,2,2,8,32]{5,4,3,2,0,1:T(8,128)(2,1)} %reshape.300), kind=kOutput, calls=%fused_computation.62 | convolution fusion | flops 1108361472 | bytes 5435936 | tf_op jit(solution)/shard_map/sgmcfl,sngl->smcfn/dot_general | solution.py:72
  117.5 5.1 %collective-permute-start = (bf16[24,2,2,8,683]{4,3,2,1,0:T(8,128)(2,1)}, bf16[24,2,2,8,683]{4,3,2,1,0:T(8,128)(2,1)S(1)}, u32[]{:S(2)}, u32[]{:S(2)}) collective-permute-start(bf16[24,2,2,8,683]{4,3,2,1,0:T(8,128)(2,1)} %bitcast_convert_fusion), channel_id=1, source_target_pairs={{0,32},{32,64},{64,96},{96,128},{128,160},{160,192},{192,224},{1,3... | collective-permute-start | bytes 3147272 | tf_op jit(solution)/shard_map/ppermute | solution.py:19
  122.6 2.1 %collective-permute-start.1 = (bf16[24,2,2,8,683]{4,3,2,1,0:T(8,128)(2,1)}, bf16[24,2,2,8,683]{4,3,2,1,0:T(8,128)(2,1)S(1)}, u32[]{:S(2)}, u32[]{:S(2)}) collective-permute-start(bf16[24,2,2,8,683]{4,3,2,1,0:T(8,128)(2,1)} %bitcast_convert_fusion), channel_id=1, source_target_pairs={{32,0},{64,32},{96,64},{128,96},{160,128},{192,160},{224,192},{33,... | collective-permute-start | bytes 3147272 | tf_op jit(solution)/shard_map/ppermute | solution.py:22
  124.8 0.1 subtract_add_fusion
  124.9 11.6 %multiply_convert_fusion.6 = (bf16[683,1024]{1,0:T(8,128)(2,1)S(1)}, bf16[683,1024]{1,0:T(8,128)(2,1)S(1)}) fusion(s32[1024]{0:T(1024)S(1)} %multiply_add_fusion.1), kind=kLoop, calls=%fused_computation.56 | loop fusion | flops 12589056 | bytes 2801664 | tf_op jit(solution)/shard_map/convert_element_type | solution.py:44
  136.4 0.0 copy-start.6
  136.5 0.0 collective-permute-done
  136.5 3.9 %collective-permute-done.1 = bf16[24,2,2,8,683]{4,3,2,1,0:T(8,128)(2,1)S(1)} collective-permute-done((bf16[24,2,2,8,683]{4,3,2,1,0:T(8,128)(2,1)}, bf16[24,2,2,8,683]{4,3,2,1,0:T(8,128)(2,1)S(1)}, u32[]{:S(2)}, u32[]{:S(2)}) %collective-permute-start.1) | collective-permute-done | bytes 1049120 | tf_op jit(solution)/shard_map/ppermute | solution.py:22
  140.4 1.5 pad_maximum_fusion
  141.9 2.6 %fusion.42 = bf16[24,2,2,8,683]{4,1,3,2,0:T(2,128)(2,1)S(1)} fusion(bf16[24,6,2,8,683]{4,3,2,1,0:T(8,128)(2,1)S(1)} %pad_maximum_fusion, bf16[24,2,2,8,683]{4,3,2,1,0:T(8,128)(2,1)S(1)} %copy-done.6, f32[24,683]{1,0:T(8,128)S(1)} %get-tuple-element.16, s32[2]{0:T(128)S(1)} %subtract_add_fusion), kind=kOutput, calls=%fused_computation.61 | convolution fusion | flops 8392716 | bytes 5311016 | tf_op jit(solution)/shard_map/ip,spcfn->sicfn/dot_general | solution.py:82
  144.5 0.2 copy.26
  144.7 0.0 copy-start.2
  144.7 8.1 %fusion.50 = bf16[24,2,2,8,1024]{4,3,2,1,0:T(8,128)(2,1)} fusion(bf16[24,2,2,8,683]{4,3,2,1,0:T(8,128)(2,1)S(1)} %copy.26, pred[24]{0:T(512)(128)(4,1)S(1)} %fusion.64, pred[24,683]{1,0:T(8,128)(4,1)S(1)} %get-tuple-element.17, bf16[683,1024]{1,0:T(8,128)(2,1)S(1)} %get-tuple-element.15, bf16[683,1024]{1,0:T(8,128)(2,1)S(1)} %get-tuple-element.14), kind=kOutput, calls=%fused_computation.65 | convolution fusion | flops 1108623360 | bytes 5435936 | tf_op jit(solution)/shard_map/sicfn,snj->sicfj/dot_general | solution.py:92
  (12 shorter events, 0.0 us)
Async XLA Ops:
  1.3 28.0 %copy-start.4 = (bf16[2,8,32,2048]{3,2,1,0:T(8,128)(2,1)S(1)}, bf16[2,8,32,2048]{3,2,1,0:T(8,128)(2,1)}, u32[]{:S(2)}) copy-start(bf16[2,8,32,2048]{3,2,1,0:T(8,128)(2,1)} %param.6) | copy-start | bytes 6291460
  1.3 28.0 %copy-start.5 = (bf16[2,8,32,2048]{3,2,1,0:T(8,128)(2,1)S(1)}, bf16[2,8,32,2048]{3,2,1,0:T(8,128)(2,1)}, u32[]{:S(2)}) copy-start(bf16[2,8,32,2048]{3,2,1,0:T(8,128)(2,1)} %param.5) | copy-start | bytes 6291460
  38.0 50.0 %all-to-all-start = ((bf16[32,2,12288]{2,1,0:T(2,128)(2,1)}), bf16[32,2,12288]{2,1,0:T(2,128)(2,1)}, u32[]{:S(2)}, u32[]{:S(2)}) async-start(bf16[32,2,12288]{2,1,0:T(2,128)(2,1)} %reshape.301), calls=%async_computation | async-start | bytes 3145728 | tf_op jit(solution)/shard_map/all_to_all | solution.py:64
  98.1 8.5 %copy-start = (bf16[683,32,32]{0,2,1:T(8,128)(2,1)S(1)}, bf16[683,32,32]{0,2,1:T(8,128)(2,1)}, u32[]{:S(2)}) copy-start(bf16[683,32,32]{0,2,1:T(8,128)(2,1)} %get-tuple-element.10) | copy-start | bytes 4196356
  98.1 8.5 %copy-start.1 = (bf16[683,32,32]{0,2,1:T(8,128)(2,1)S(1)}, bf16[683,32,32]{0,2,1:T(8,128)(2,1)}, u32[]{:S(2)}) copy-start(bf16[683,32,32]{0,2,1:T(8,128)(2,1)} %get-tuple-element.11) | copy-start | bytes 4196356
  106.7 18.1 %copy-start.3 = (s32[16]{0:T(128)S(1)}, s32[16]{0:T(128)}, u32[]{:S(2)}) copy-start(s32[16]{0:T(128)} %param.8) | copy-start | bytes 196
  117.5 19.0 %collective-permute-start = (bf16[24,2,2,8,683]{4,3,2,1,0:T(8,128)(2,1)}, bf16[24,2,2,8,683]{4,3,2,1,0:T(8,128)(2,1)S(1)}, u32[]{:S(2)}, u32[]{:S(2)}) collective-permute-start(bf16[24,2,2,8,683]{4,3,2,1,0:T(8,128)(2,1)} %bitcast_convert_fusion), channel_id=1, source_target_pairs={{0,32},{32,64},{64,96},{96,128},{128,160},{160,192},{192,224},{1,3... | collective-permute-start | bytes 3147272 | tf_op jit(solution)/shard_map/ppermute | solution.py:19
  122.6 17.7 %collective-permute-start.1 = (bf16[24,2,2,8,683]{4,3,2,1,0:T(8,128)(2,1)}, bf16[24,2,2,8,683]{4,3,2,1,0:T(8,128)(2,1)S(1)}, u32[]{:S(2)}, u32[]{:S(2)}) collective-permute-start(bf16[24,2,2,8,683]{4,3,2,1,0:T(8,128)(2,1)} %bitcast_convert_fusion), channel_id=1, source_target_pairs={{32,0},{64,32},{96,64},{128,96},{160,128},{192,160},{224,192},{33,... | collective-permute-start | bytes 3147272 | tf_op jit(solution)/shard_map/ppermute | solution.py:22
  136.4 5.4 %copy-start.6 = (bf16[24,2,2,8,683]{4,3,2,1,0:T(8,128)(2,1)S(1)}, bf16[24,2,2,8,683]{4,3,2,1,0:T(8,128)(2,1)}, u32[]{:S(2)}) copy-start(bf16[24,2,2,8,683]{4,3,2,1,0:T(8,128)(2,1)} %param.9) | copy-start | bytes 3147268
  144.7 8.1 %copy-start.2 = (bf16[24,2,2,8,683]{4,3,2,1,0:T(8,128)(2,1)}, bf16[24,2,2,8,683]{4,3,2,1,0:T(8,128)(2,1)S(1)}, u32[]{:S(2)}) copy-start(bf16[24,2,2,8,683]{4,3,2,1,0:T(8,128)(2,1)S(1)} %copy.26) | copy-start | bytes 3147268
where the time goes:
time: 153 us
  other arithmetic  59.6 us (39%)
  waiting for transfers between devices  25.8 us (17%)
  matrix products  25 us (16%)
  local copies, waits for them, and re-layouts  22.1 us (14%)
  starting transfers between devices  19.6 us (13%)
    another operation x1, other arithmetic  28 us
    convert_element_type x2, other arithmetic, meridional_table(): odd_table = (jnp.sin(angle) * factor).astype(jnp.bfloat16)  26.5 us
    all_to_all x1, waiting for transfers between devices, per_device(): lax.all_to_all(outgoing, 'lat', split_axis=0, concat_axis=1, tiled=True)  21.9 us
    unnamed x19, local copies, waits for them, and re-layouts  12.9 us
    all_to_all x1, starting transfers between devices, per_device(): lax.all_to_all(outgoing, 'lat', split_axis=0, concat_axis=1, tiled=True)  12.3 us
    dot_general x1, matrix products, forward(): jnp.einsum('sgmcfl,sngl->smcfn', coefficients, basis_split, preferred_ele...  10.8 us
    reshape x1, local copies, waits for them, and re-layouts, per_device(): received.reshape(slots_here, lat_count, mem_local, 2, field_count, lat_lo...  8.53 us
    dot_general x1, matrix products, per_device(): jnp.einsum('sicfn,snj->sicfj', children, basis, preferred_element_type=jn...  8.08 us
  transfers between devices with their start and end apart: 3, of which 2 were waited for; matrix products, arithmetic and copies ran while one was open for 18% of the time, Pallas kernels for 0%

commit v1 on v0

v1 whole, which is shorter than its diff:
```python
import functools
import math

import jax
import jax.numpy as jnp
from jax import lax
from jax.experimental import pallas as pl
from jax.experimental.pallas import tpu as pltpu
from jax.sharding import PartitionSpec as P

NLAT = 1024
NLON = 2048
TRUNC = 683
NPAD = 768
SPREAD = 2
SG = 8
MESH = pl.DeviceIdType.MESH
F32 = jnp.float32
BF16 = jnp.bfloat16
NT = (((1,), (1,)), ((), ()))
NN = (((1,), (0,)), ((), ()))


def iota(shape, dim):
    return lax.broadcasted_iota(jnp.int32, shape, dim)


def cos_sin(phase, period):
    eighth = period // 8
    quarter = period // 4
    shifted = phase + eighth
    quad = (shifted // quarter) & 3
    x = ((shifted & (quarter - 1)) - eighth).astype(F32) * (2.0 * math.pi / period)
    y = x * x
    s = x * (1.0 + y * (-1.0 / 6 + y * (1.0 / 120 + y * (-1.0 / 5040 + y * (1.0 / 362880)))))
    c = 1.0 + y * (-0.5 + y * (1.0 / 24 + y * (-1.0 / 720 + y * (1.0 / 40320))))
    odd = (quad & 1) == 1
    cos = jnp.where(odd, s, c)
    sin = jnp.where(odd, c, s)
    cos = jnp.where((quad == 1) | (quad == 2), -cos, cos)
    sin = jnp.where(quad >= 2, -sin, sin)
    return cos, sin


def kernel(
    lat_count, member_count,
    parents, waves, waves_row, velocity, tracer, noise,
    spectra_out, fourier_out,
    wave_b, vel, tra, prod, table, four, low, high, sel, recv, even_t, odd_t,
    xmat, spec, kids, noise_v, spec_v, four_v,
    in_sem, noise_sem, xs_sem, xr_sem, as_sem, ar_sem, out_sem,
):
    me = lax.axis_index("lat")
    group = lax.axis_index("member")
    chunks = four.shape[0]
    slots_here = chunks * SG
    lat_local = NLAT // lat_count
    mf = vel.shape[0] // lat_local
    fields = mf // 2

    barrier = pltpu.get_barrier_semaphore()
    up = lax.rem(group + 1, member_count)
    down = lax.rem(group + member_count - 1, member_count)

    load_v = pltpu.make_async_copy(velocity, vel, in_sem.at[0])
    load_t = pltpu.make_async_copy(tracer, tra, in_sem.at[1])
    load_v.start()
    load_t.start()

    @pl.loop(1, lat_count)
    def _(o):
        pl.semaphore_signal(
            barrier, inc=1, device_id={"lat": lax.rem(me + o, lat_count)}, device_id_type=MESH
        )

    pl.semaphore_signal(barrier, inc=1, device_id={"member": up}, device_id_type=MESH)
    pl.semaphore_signal(barrier, inc=1, device_id={"member": down}, device_id_type=MESH)
    load_n = pltpu.make_async_copy(noise, noise_v, noise_sem)
    load_n.start()

    for r in range(waves_row.shape[0]):
        row = waves_row[r : r + 1, :].astype(F32)
        wave_b[128 * r : 128 * r + 128, :] = jnp.transpose(jnp.broadcast_to(row, (128, 128)))

    def make_table(q):
        @pl.loop(0, lat_count)
        def _(d):
            w = wave_b[pl.ds(pl.multiple_of(d * slots_here + q * SG, SG), SG), :].astype(jnp.int32)
            c, s = cos_sin((w * iota((SG, 128), 1)) & (NLON - 1), NLON)
            ct, st = cos_sin((w * 128) & (NLON - 1), NLON)
            weight = jnp.where(w < TRUNC, 1.0 / math.sqrt(NLON), 0.0)
            c = c * weight
            s = -s * weight
            sign = jnp.where((w & 1) == 1, -1.0, 1.0)
            rows = pl.ds(pl.multiple_of(d * 2 * SG, 2 * SG), 2 * SG)
            half = NLON // 2
            for t in range(half // 128):
                here = jnp.concatenate([c, s], axis=0)
                there = jnp.concatenate([c * sign, s * sign], axis=0)
                table[rows, 128 * t : 128 * t + 128] = here.astype(BF16)
                table[rows, half + 128 * t : half + 128 * t + 128] = there.astype(BF16)
                if t + 1 < half // 128:
                    c, s = c * ct + s * st, s * ct - c * st

    def zonal(q):
        make_table(q)
        per = 16

        @pl.loop(0, lat_count // per)
        def _(b):
            rows = pl.ds(pl.multiple_of(b * per * 2 * SG, per * 2 * SG), per * 2 * SG)
            out = lax.dot_general(table[rows, :], prod[...], NT, preferred_element_type=F32)
            four[q, pl.ds(b * per, per)] = out.astype(BF16).reshape(per, 2 * SG, out.shape[1])

    load_v.wait()
    load_t.wait()

    @pl.loop(0, vel.shape[0] // 16)
    def _(b):
        rows = pl.ds(pl.multiple_of(b * 16, 16), 16)
        prod[rows, :] = (vel[rows, :].astype(F32) * tra[rows, :].astype(F32)).astype(BF16)

    def x_copies(q):
        to_up = pltpu.make_async_remote_copy(
            src_ref=four.at[q], dst_ref=low.at[q], send_sem=xs_sem.at[q, 0], recv_sem=xr_sem.at[q, 0],
            device_id={"member": up}, device_id_type=MESH,
        )
        to_down = pltpu.make_async_remote_copy(
            src_ref=four.at[q], dst_ref=high.at[q], send_sem=xs_sem.at[q, 1], recv_sem=xr_sem.at[q, 1],
            device_id={"member": down}, device_id_type=MESH,
        )
        return to_up, to_down

    def a_copy(q, target):
        return pltpu.make_async_remote_copy(
            src_ref=sel.at[q, target], dst_ref=recv.at[q, me],
            send_sem=as_sem.at[q], recv_sem=ar_sem.at[q],
            device_id={"lat": target}, device_id_type=MESH,
        )

    zonal(0)
    pl.semaphore_wait(barrier, lat_count + 1)
    for c in x_copies(0):
        c.start()
    for q in range(1, chunks):
        zonal(q)
        for c in x_copies(q):
            c.start()

    def make_basis():
        step = 64
        half_turn = 2 * NLAT
        lanes = 128

        @pl.loop(0, NLAT // lanes)
        def _(jt):
            j = jt * lanes + iota((8, lanes), 1)
            sub = iota((8, lanes), 0)
            c8, s8 = cos_sin((8 * (2 * j + 1)) & (2 * half_turn - 1), 2 * half_turn)
            cols = pl.ds(pl.multiple_of(jt * lanes, lanes), lanes)
            scale = math.sqrt(2.0 / NLAT)

            @pl.loop(0, NPAD // step)
            def _(a):
                n = a * step + sub
                c, s = cos_sin((n * (2 * j + 1)) & (2 * half_turn - 1), 2 * half_turn)
                c = c * scale
                s = s * scale
                for b in range(step // 16):
                    c2, s2 = c * c8 - s * s8, s * c8 + c * s8
                    n16 = pl.ds(pl.multiple_of(a * step + b * 16, 16), 16)
                    even_t[n16, cols] = jnp.concatenate([c, c2], axis=0).astype(BF16)
                    odd_t[n16, cols] = jnp.concatenate([s, s2], axis=0).astype(BF16)
                    c, s = c2 * c8 - s2 * s8, s2 * c8 + c2 * s8

    make_basis()

    first = group * 2
    for q in range(chunks):
        for c in x_copies(q):
            c.wait_recv()
        halves = mf // 2 * lat_local
        for m in range(2):
            place = parents[first + m] - first + SPREAD

            @pl.loop(0, lat_count)
            def _(d):
                chosen = None
                for p in range(m, m + 2 * SPREAD + 1):
                    source = (low, four, high)[p // 2]
                    cand = source[q, d, :, (p % 2) * halves : (p % 2 + 1) * halves]
                    hit = jnp.broadcast_to(place == p, cand.shape)
                    chosen = cand if chosen is None else jnp.where(hit, cand, chosen)
                sel[q, d, :, m * halves : (m + 1) * halves] = chosen

        @pl.loop(1, lat_count)
        def _(o):
            a_copy(q, lax.rem(me + o, lat_count)).start()

        recv[q, me] = sel[q, me]

    load_n.wait()
    kids[...] = jnp.zeros_like(kids)

    for q in range(chunks):
        pltpu.make_async_remote_copy(
            src_ref=recv.at[q, pl.ds(0, lat_count - 1)], dst_ref=recv.at[q, pl.ds(0, lat_count - 1)],
            send_sem=as_sem.at[q], recv_sem=ar_sem.at[q], device_id={"lat": me}, device_id_type=MESH,
        ).wait_recv()
        lane = iota((2 * SG, 128), 1)
        per = 128 // lat_local
        for t in range(mf // per):
            @pl.loop(0, lat_count // per)
            def _(p):
                cols = slice(128 * t, 128 * t + 128)
                parts = [recv[q, p * per + i, :, cols] for i in range(per)]
                for k in range(per):
                    xmat[pl.ds((t * per + k) * 2 * SG, 2 * SG), pl.ds(pl.multiple_of(p * 128, 128), 128)] = (
                        jnp.concatenate([a[:, k * lat_local : (k + 1) * lat_local] for a in parts], axis=1)
                    )
        w = wave_b[pl.ds(pl.multiple_of(me * slots_here + q * SG, SG), SG), :].astype(jnp.int32)
        x = xmat[...]
        for nt in range(NPAD // 256):
            cols = slice(256 * nt, 256 * nt + 256)
            even = lax.dot_general(x, even_t[cols, :], NT, preferred_element_type=F32)
            odd = lax.dot_general(x, odd_t[cols, :], NT, preferred_element_type=F32)
            for half in range(2):
                n = 256 * nt + 128 * half + iota((SG, 128), 1)
                live = (n >= w) & (w < TRUNC) & (n < TRUNC)
                is_odd = (w & 1) == 1
                lanes = slice(128 * half, 128 * half + 128)
                for i in range(mf * 2):
                    member, field, part = i // (2 * fields), i // 2 % fields, i % 2
                    rows = slice(SG * i, SG * i + SG)
                    value = jnp.where(is_odd, odd[rows, lanes], even[rows, lanes])
                    value = jnp.where(live, value, 0.0)
                    start = member * 2 * fields + part * fields + field
                    start = start + (2 * nt + half) * SG * 2 * mf
                    spec[pl.ds(start, SG, stride=2 * mf), :] = value

        for s in range(SG):
            wave = waves[me * slots_here + q * SG + s]
            rows = slice(s * 2 * mf, (s + 1) * 2 * mf)
            out_rows = slice((q * SG + s) * 2 * mf, (q * SG + s + 1) * 2 * mf)
            n = iota((2 * mf, TRUNC), 1)
            live = (n >= wave) & (wave < TRUNC)
            base = jnp.concatenate(
                [spec[pl.ds((t * SG + s) * 2 * mf, 2 * mf), :] for t in range(NPAD // 128)], axis=1
            )[:, :TRUNC].astype(BF16).astype(F32)
            extra = noise_v[out_rows, :].astype(F32)
            child = (base + jnp.where(live, extra, 0.0)).astype(BF16)
            spec_v[out_rows, :] = child
            kids[rows, :TRUNC] = child

        for nt in range(NLAT // 256):
            cols = slice(256 * nt, 256 * nt + 256)
            even = lax.dot_general(kids[...], even_t[:, cols], NN, preferred_element_type=F32)
            odd = lax.dot_general(kids[...], odd_t[:, cols], NN, preferred_element_type=F32)
            for s in range(SG):
                wave = waves[me * slots_here + q * SG + s]
                rows = slice(s * 2 * mf, (s + 1) * 2 * mf)
                is_odd = jnp.broadcast_to((wave & 1) == 1, (2 * mf, 256))
                value = jnp.where(is_odd, odd[rows], even[rows])
                four_v[q * SG * 2 * mf + s * 2 * mf : q * SG * 2 * mf + (s + 1) * 2 * mf, cols] = value.astype(BF16)

        block = pl.ds(q * SG * 2 * mf, SG * 2 * mf)
        pltpu.make_async_copy(spec_v.at[block], spectra_out.at[block], out_sem.at[q, 0]).start()
        pltpu.make_async_copy(four_v.at[block], fourier_out.at[block], out_sem.at[q, 1]).start()

    for q in range(chunks):
        for c in x_copies(q):
            c.wait_send()
        pltpu.make_async_remote_copy(
            src_ref=sel.at[q, pl.ds(0, lat_count - 1)], dst_ref=recv.at[q, pl.ds(0, lat_count - 1)],
            send_sem=as_sem.at[q], recv_sem=ar_sem.at[q], device_id={"lat": me}, device_id_type=MESH,
        ).wait_send()
        block = pl.ds(q * SG * 2 * mf, SG * 2 * mf)
        pltpu.make_async_copy(spec_v.at[block], spectra_out.at[block], out_sem.at[q, 0]).wait()
        pltpu.make_async_copy(four_v.at[block], fourier_out.at[block], out_sem.at[q, 1]).wait()


def per_device(lat_count, member_count, velocity, tracer, wave_slots, parents, noise):
    mem, fields, lat_local, lon = velocity.shape
    slots = wave_slots.shape[0]
    here = slots // lat_count
    chunks = here // SG
    rows = mem * fields * lat_local
    mf = mem * fields
    out_rows = here * mem * 2 * fields
    chunk_rows = SG * 2 * mf
    any_spec = pl.BlockSpec(memory_space=pl.ANY)
    smem = pl.BlockSpec(memory_space=pltpu.SMEM)
    vmem = pl.BlockSpec(memory_space=pltpu.VMEM)
    msg = (chunks, lat_count, 2 * SG, rows)
    dma = pltpu.SemaphoreType.DMA
    spectra, fourier = pl.pallas_call(
        functools.partial(kernel, lat_count, member_count),
        out_shape=(
            jax.ShapeDtypeStruct((out_rows, TRUNC), BF16),
            jax.ShapeDtypeStruct((out_rows, NLAT), BF16),
        ),
        in_specs=[smem, smem, vmem, any_spec, any_spec, any_spec],
        out_specs=(any_spec, any_spec),
        scratch_shapes=[
            pltpu.VMEM((slots, 128), F32),
            pltpu.VMEM((rows, lon), BF16),
            pltpu.VMEM((rows, lon), BF16),
            pltpu.VMEM((rows, lon), BF16),
            pltpu.VMEM((lat_count * 2 * SG, lon), BF16),
            pltpu.VMEM(msg, BF16),
            pltpu.VMEM(msg, BF16),
            pltpu.VMEM(msg, BF16),
            pltpu.VMEM(msg, BF16),
            pltpu.VMEM(msg, BF16),
            pltpu.VMEM((NPAD, NLAT), BF16),
            pltpu.VMEM((NPAD, NLAT), BF16),
            pltpu.VMEM((chunk_rows, NLAT), BF16),
            pltpu.VMEM((NPAD // 128 * chunk_rows, 128), F32),
            pltpu.VMEM((chunk_rows, NPAD), BF16),
            pltpu.VMEM((out_rows, TRUNC), BF16),
            pltpu.VMEM((out_rows, TRUNC), BF16),
            pltpu.VMEM((out_rows, NLAT), BF16),
            dma((2,)),
            dma,
            dma((chunks, 2)),
            dma((chunks, 2)),
            dma((chunks,)),
            dma((chunks,)),
            dma((chunks, 2)),
        ],
        compiler_params=pltpu.CompilerParams(
            collective_id=0, has_side_effects=True, vmem_limit_bytes=60 * 1024 * 1024
        ),
        name="transform",
    )(
        parents,
        wave_slots,
        wave_slots.reshape(slots // 128, 128),
        velocity.reshape(rows, lon),
        tracer.reshape(rows, lon),
        noise.reshape(out_rows, TRUNC),
    )
    return (
        spectra.reshape(here, mem, 2, fields, TRUNC),
        fourier.reshape(here, mem, 2, fields, NLAT),
    )


def solution(mesh):
    in_specs = (
        P("member", None, "lat", None),
        P("member", None, "lat", None),
        P(),
        P(),
        P("lat", "member", None, None, None),
    )
    out_specs = (P("lat", "member", None, None, None), P("lat", "member", None, None, None))
    return jax.shard_map(
        functools.partial(per_device, mesh.shape["lat"], mesh.shape["member"]),
        mesh=mesh, in_specs=in_specs, out_specs=out_specs, check_vma=False,
    )
```

time: 153 us -> 70.9 us (0.46)
  the two profiles are of different devices: /device:TPU:1 before, /device:TPU:14 now
where the time goes in v1:
time: 70.9 us; the launch traced here: 70.8 us
  Pallas kernels  66.5 us (94%)
  local copies, waits for them, and re-layouts  3.62 us (5%)
    pallas_call x1, Pallas kernels, per_device(): pl.pallas_call(functools.partial(kernel, lat_count, member_count), out_sh...  66.5 us
    unnamed x4, local copies, waits for them, and re-layouts  3.62 us

profile of v1, /device:TPU:14, one launch (start us, length us, event | category | flops | bytes accessed | tf_op | source)
XLA Modules:
  0.0 70.8 jit_solution(7189836223373096263)
XLA Ops:
  0.6 66.5 %transform.1 = (bf16[768,683]{1,0:T(8,128)(2,1)}, bf16[768,1024]{1,0:T(8,128)(2,1)}) custom-call(s32[16]{0:T(128)} %parents.1, s32[768]{0:T(1024)} %waves.1, s32[6,128]{1,0:T(8,128)} %bitcast.11, bf16[512,2048]{1,0:T(8,128)(2,1)} %bitcast.6, bf16[512,2048]{1,0:T(8,128)(2,1)} %bitcast.7, bf16[768,683]{1,0:T(8,128)(2,1)} %bitcast.10), custom_call_target="tpu_custom_call" | custom-call | tf_op jit(solution)/shard_map/transform/pallas_call | solution.py:296
  67.2 0.0 copy-start
  67.2 2.5 %copy.9 = bf16[24,2,2,8,683]{4,3,2,1,0:T(8,128)(2,1)} copy(bf16[24,2,2,8,683]{4,3,2,1,0:T(8,128)(2,1)} %bitcast.9) | data formatting | bytes 2098176
  69.7 0.0 copy-done
  69.7 1.1 %copy.10 = bf16[24,2,2,8,1024]{4,3,2,1,0:T(8,128)(2,1)} copy(bf16[24,2,2,8,1024]{4,3,2,1,0:T(8,128)(2,1)S(1)} %bitcast.8) | data formatting | bytes 3145728
Async XLA Ops:
  67.2 2.5 %copy-start = (bf16[768,1024]{1,0:T(8,128)(2,1)S(1)}, bf16[768,1024]{1,0:T(8,128)(2,1)}, u32[]{:S(2)}) copy-start(bf16[768,1024]{1,0:T(8,128)(2,1)} %get-tuple-element.5) | copy-start | bytes 4718596

commit v2 on v1

--- a/solution.py
+++ b/solution.py
@@ -44,16 +44,18 @@
 
 def kernel(
     lat_count, member_count,
-    parents, waves, waves_row, velocity, tracer, noise,
+    parents_hbm, waves_hbm, waves_row_hbm, velocity, tracer, noise,
     spectra_out, fourier_out,
-    wave_b, vel, tra, prod, table, four, low, high, sel, recv, even_t, odd_t,
-    xmat, spec, kids, noise_v, spec_v, four_v,
-    in_sem, noise_sem, xs_sem, xr_sem, as_sem, ar_sem, out_sem,
+    parents, waves, waves_row, wave_b, vel, tra, prod, table, four, low, high, sel, recv, even_t, odd_t,
+    xmat, spec, kids, noise_v, spec_v, four_v, own_s, low_s, high_s,
+    small_sem, ss_sem, sr_sem, in_sem, noise_sem, xs_sem, xr_sem, as_sem, ar_sem, out_sem,
 ):
     me = lax.axis_index("lat")
     group = lax.axis_index("member")
     chunks = four.shape[0]
     slots_here = chunks * SG
+    halves = 2
+    half_count = lat_count // halves
     lat_local = NLAT // lat_count
     mf = vel.shape[0] // lat_local
     fields = mf // 2
@@ -61,11 +63,6 @@
     barrier = pltpu.get_barrier_semaphore()
     up = lax.rem(group + 1, member_count)
     down = lax.rem(group + member_count - 1, member_count)
-
-    load_v = pltpu.make_async_copy(velocity, vel, in_sem.at[0])
-    load_t = pltpu.make_async_copy(tracer, tra, in_sem.at[1])
-    load_v.start()
-    load_t.start()
 
     @pl.loop(1, lat_count)
     def _(o):
@@ -75,42 +72,75 @@
 
     pl.semaphore_signal(barrier, inc=1, device_id={"member": up}, device_id_type=MESH)
     pl.semaphore_signal(barrier, inc=1, device_id={"member": down}, device_id_type=MESH)
+    load_w = pltpu.make_async_copy(waves_row_hbm, waves_row, small_sem.at[0])
+    load_w.start()
+    load_v = pltpu.make_async_copy(velocity, vel, in_sem.at[0])
+    load_t = pltpu.make_async_copy(tracer, tra, in_sem.at[1])
+    load_v.start()
+    load_t.start()
+    load_s = pltpu.make_async_copy(waves_hbm, waves, small_sem.at[1])
+    load_s.start()
+    load_p = pltpu.make_async_copy(parents_hbm, parents, small_sem.at[2])
+    load_p.start()
     load_n = pltpu.make_async_copy(noise, noise_v, noise_sem)
     load_n.start()
+    load_w.wait()
 
     for r in range(waves_row.shape[0]):
         row = waves_row[r : r + 1, :].astype(F32)
         wave_b[128 * r : 128 * r + 128, :] = jnp.transpose(jnp.broadcast_to(row, (128, 128)))
 
-    def make_table(q):
-        @pl.loop(0, lat_count)
-        def _(d):
-            w = wave_b[pl.ds(pl.multiple_of(d * slots_here + q * SG, SG), SG), :].astype(jnp.int32)
-            c, s = cos_sin((w * iota((SG, 128), 1)) & (NLON - 1), NLON)
+    y_count = 128 // lat_local
+    z_count = lat_count // y_count
+    my_z, my_y = me // y_count, lax.rem(me, y_count)
+
+    def turn_of(k):
+        r = z_count - 1 - k
+        return (r + 1) // 2 * (1 - 2 * lax.rem(r + 1, 2))
+
+    def target_of(i):
+        z = lax.rem(my_z + turn_of(i // y_count) + z_count, z_count)
+        return z * y_count + lax.rem(my_y + i + 1, y_count)
+
+    def make_table(q, first):
+        together = 4
+
+        @pl.loop(0, half_count // together)
+        def _(b):
+            w = jnp.concatenate(
+                [
+                    wave_b[
+                        pl.ds(pl.multiple_of(target_of(first + b * together + j) * slots_here + q * SG, SG), SG), :
+                    ]
+                    for j in range(together)
+                ],
+                axis=0,
+            ).astype(jnp.int32)
+            c, s = cos_sin((w * iota(w.shape, 1)) & (NLON - 1), NLON)
             ct, st = cos_sin((w * 128) & (NLON - 1), NLON)
             weight = jnp.where(w < TRUNC, 1.0 / math.sqrt(NLON), 0.0)
             c = c * weight
             s = -s * weight
             sign = jnp.where((w & 1) == 1, -1.0, 1.0)
-            rows = pl.ds(pl.multiple_of(d * 2 * SG, 2 * SG), 2 * SG)
             half = NLON // 2
             for t in range(half // 128):
-                here = jnp.concatenate([c, s], axis=0)
-                there = jnp.concatenate([c * sign, s * sign], axis=0)
-                table[rows, 128 * t : 128 * t + 128] = here.astype(BF16)
-                table[rows, half + 128 * t : half + 128 * t + 128] = there.astype(BF16)
+                for factor, offset in ((None, 0), (sign, half)):
+                    cc = c if factor is None else c * factor
+                    ss = s if factor is None else s * factor
+                    for j in range(together):
+                        part = slice(j * SG, j * SG + SG)
+                        rows = pl.ds(pl.multiple_of((b * together + j) * 2 * SG, 2 * SG), 2 * SG)
+                        table[rows, offset + 128 * t : offset + 128 * t + 128] = jnp.concatenate(
+                            [cc[part], ss[part]], axis=0
+                        ).astype(BF16)
                 if t + 1 < half // 128:
                     c, s = c * ct + s * st, s * ct - c * st
 
-    def zonal(q):
-        make_table(q)
-        per = 16
-
-        @pl.loop(0, lat_count // per)
-        def _(b):
-            rows = pl.ds(pl.multiple_of(b * per * 2 * SG, per * 2 * SG), per * 2 * SG)
-            out = lax.dot_general(table[rows, :], prod[...], NT, preferred_element_type=F32)
-            four[q, pl.ds(b * per, per)] = out.astype(BF16).reshape(per, 2 * SG, out.shape[1])
+    def zonal(q, h):
+        first = h * half_count
+        make_table(q, first)
+        out = lax.dot_general(table[...], prod[...], NT, preferred_element_type=F32)
+        four[q, first : first + half_count] = out.astype(BF16).reshape(half_count, 2 * SG, out.shape[1])
 
     load_v.wait()
     load_t.wait()
@@ -120,32 +150,45 @@
         rows = pl.ds(pl.multiple_of(b * 16, 16), 16)
         prod[rows, :] = (vel[rows, :].astype(F32) * tra[rows, :].astype(F32)).astype(BF16)
 
-    def x_copies(q):
+    def x_copies(q, h):
+        block = pl.ds(h * half_count, half_count)
         to_up = pltpu.make_async_remote_copy(
-            src_ref=four.at[q], dst_ref=low.at[q], send_sem=xs_sem.at[q, 0], recv_sem=xr_sem.at[q, 0],
+            src_ref=four.at[q, block], dst_ref=low.at[q, block],
+            send_sem=xs_sem.at[q, h, 0], recv_sem=xr_sem.at[q, h, 0],
             device_id={"member": up}, device_id_type=MESH,
         )
         to_down = pltpu.make_async_remote_copy(
-            src_ref=four.at[q], dst_ref=high.at[q], send_sem=xs_sem.at[q, 1], recv_sem=xr_sem.at[q, 1],
+            src_ref=four.at[q, block], dst_ref=high.at[q, block],
+            send_sem=xs_sem.at[q, h, 1], recv_sem=xr_sem.at[q, h, 1],
             device_id={"member": down}, device_id_type=MESH,
         )
         return to_up, to_down
 
-    def a_copy(q, target):
-        return pltpu.make_async_remote_copy(
-            src_ref=sel.at[q, target], dst_ref=recv.at[q, me],
-            send_sem=as_sem.at[q], recv_sem=ar_sem.at[q],
-            device_id={"lat": target}, device_id_type=MESH,
-        )
-
-    zonal(0)
+    def send_half(q, h, source):
+        first = h * half_count
+        last = h == halves - 1
+
+        @pl.loop(first, first + half_count - (1 if last else 0))
+        def _(i):
+            pltpu.make_async_remote_copy(
+                src_ref=source.at[q, i], dst_ref=recv.at[q, me],
+                send_sem=as_sem.at[q], recv_sem=ar_sem.at[q, my_z],
+                device_id={"lat": target_of(i)}, device_id_type=MESH,
+            ).start()
+
+        if last:
+            recv[q, me] = source[q, lat_count - 1]
+
+    zonal(0, 0)
     pl.semaphore_wait(barrier, lat_count + 1)
-    for c in x_copies(0):
-        c.start()
+    send_half(0, 0, four)
+    zonal(0, 1)
+    send_half(0, 1, four)
     for q in range(1, chunks):
-        zonal(q)
-        for c in x_copies(q):
-            c.start()
+        for h in range(halves):
+            zonal(q, h)
+            for c in x_copies(q, h):
+                c.start()
 
     def make_basis():
         step = 64
@@ -173,51 +216,82 @@
                     odd_t[n16, cols] = jnp.concatenate([s, s2], axis=0).astype(BF16)
                     c, s = c2 * c8 - s2 * s8, s2 * c8 + c2 * s8
 
-    make_basis()
-
-    first = group * 2
-    for q in range(chunks):
-        for c in x_copies(q):
-            c.wait_recv()
-        halves = mf // 2 * lat_local
-        for m in range(2):
-            place = parents[first + m] - first + SPREAD
-
-            @pl.loop(0, lat_count)
-            def _(d):
+    load_s.wait()
+    load_p.wait()
+    first_member = group * 2
+    places = [parents[first_member + m] - first_member + SPREAD for m in range(2)]
+
+    def select_half(q, h):
+        width = fields * lat_local
+
+        @pl.loop(h * half_count, (h + 1) * half_count)
+        def _(i):
+            for m in range(2):
                 chosen = None
                 for p in range(m, m + 2 * SPREAD + 1):
                     source = (low, four, high)[p // 2]
-                    cand = source[q, d, :, (p % 2) * halves : (p % 2 + 1) * halves]
-                    hit = jnp.broadcast_to(place == p, cand.shape)
+                    cand = source[q, i, :, (p % 2) * width : (p % 2 + 1) * width]
+                    hit = jnp.broadcast_to(places[m] == p, cand.shape)
                     chosen = cand if chosen is None else jnp.where(hit, cand, chosen)
-                sel[q, d, :, m * halves : (m + 1) * halves] = chosen
-
-        @pl.loop(1, lat_count)
-        def _(o):
-            a_copy(q, lax.rem(me + o, lat_count)).start()
-
-        recv[q, me] = sel[q, me]
-
+                sel[q, i, :, m * width : (m + 1) * width] = chosen
+
+    def relay(q, h):
+        for c in x_copies(q, h):
+            c.wait_recv()
+        select_half(q, h)
+        send_half(q, h, sel)
+
+    for q in range(1, chunks):
+        for h in range(halves):
+            relay(q, h)
+
+    make_basis()
     load_n.wait()
     kids[...] = jnp.zeros_like(kids)
 
-    for q in range(chunks):
+    def arrive(q, p, count):
+        block = recv.at[q, pl.ds(p * y_count, count)]
         pltpu.make_async_remote_copy(
-            src_ref=recv.at[q, pl.ds(0, lat_count - 1)], dst_ref=recv.at[q, pl.ds(0, lat_count - 1)],
-            send_sem=as_sem.at[q], recv_sem=ar_sem.at[q], device_id={"lat": me}, device_id_type=MESH,
+            src_ref=block, dst_ref=block, send_sem=as_sem.at[q], recv_sem=ar_sem.at[q, p],
+            device_id={"lat": me}, device_id_type=MESH,
         ).wait_recv()
-        lane = iota((2 * SG, 128), 1)
+
+    def shuffle(q):
         per = 128 // lat_local
-        for t in range(mf // per):
-            @pl.loop(0, lat_count // per)
-            def _(p):
-                cols = slice(128 * t, 128 * t + 128)
-                parts = [recv[q, p * per + i, :, cols] for i in range(per)]
-                for k in range(per):
-                    xmat[pl.ds((t * per + k) * 2 * SG, 2 * SG), pl.ds(pl.multiple_of(p * 128, 128), 128)] = (
-                        jnp.concatenate([a[:, k * lat_local : (k + 1) * lat_local] for a in parts], axis=1)
-                    )
+        lane = iota((2 * SG, 128), 1) // lat_local
+        low_half = lane < 2
+        even_block = (lane & 1) == 0
+
+        def swap(x, y, mask, width):
+            left = jnp.where(mask, x, pltpu.roll(y, width, 1))
+            right = jnp.where(mask, pltpu.roll(x, 128 - width, 1), y)
+            return left, right
+
+        def arrange(p):
+            target = pl.ds(pl.multiple_of(p * 128, 128), 128)
+            for t in range(mf // per):
+                x0, x1, x2, x3 = [recv[q, p * per + i, :, 128 * t : 128 * t + 128] for i in range(per)]
+                x0, x2 = swap(x0, x2, low_half, 2 * lat_local)
+                x1, x3 = swap(x1, x3, low_half, 2 * lat_local)
+                x0, x1 = swap(x0, x1, even_block, lat_local)
+                x2, x3 = swap(x2, x3, even_block, lat_local)
+                for k, x in enumerate((x0, x1, x2, x3)):
+                    xmat[(t * per + k) * 2 * SG : (t * per + k + 1) * 2 * SG, target] = x
+
+        @pl.loop(0, z_count - 1)
+        def _(k):
+            p = lax.rem(my_z - turn_of(k) + z_count, z_count)
+            arrive(q, p, per)
+            arrange(p)
+
+        arrive(q, my_z, per - 1)
+        arrange(my_z)
+
+    def forward(q):
+        shuffle(q)
+        product(q)
+
+    def product(q):
         w = wave_b[pl.ds(pl.multiple_of(me * slots_here + q * SG, SG), SG), :].astype(jnp.int32)
         x = xmat[...]
         for nt in range(NPAD // 256):
@@ -238,15 +312,14 @@
                     start = start + (2 * nt + half) * SG * 2 * mf
                     spec[pl.ds(start, SG, stride=2 * mf), :] = value
 
+    def finish(q, base_of):
         for s in range(SG):
             wave = waves[me * slots_here + q * SG + s]
             rows = slice(s * 2 * mf, (s + 1) * 2 * mf)
             out_rows = slice((q * SG + s) * 2 * mf, (q * SG + s + 1) * 2 * mf)
             n = iota((2 * mf, TRUNC), 1)
             live = (n >= wave) & (wave < TRUNC)
-            base = jnp.concatenate(
-                [spec[pl.ds((t * SG + s) * 2 * mf, 2 * mf), :] for t in range(NPAD // 128)], axis=1
-            )[:, :TRUNC].astype(BF16).astype(F32)
+            base = base_of(q, s).astype(F32)[:, :TRUNC]
             extra = noise_v[out_rows, :].astype(F32)
             child = (base + jnp.where(live, extra, 0.0)).astype(BF16)
             spec_v[out_rows, :] = child
@@ -267,12 +340,61 @@
         pltpu.make_async_copy(spec_v.at[block], spectra_out.at[block], out_sem.at[q, 0]).start()
         pltpu.make_async_copy(four_v.at[block], fourier_out.at[block], out_sem.at[q, 1]).start()
 
+    def spec_of(q, s):
+        tiles = [spec[pl.ds((t * SG + s) * 2 * mf, 2 * mf), :] for t in range(NPAD // 128)]
+        return jnp.concatenate(tiles, axis=1).astype(BF16)
+
+    def s_copies():
+        to_up = pltpu.make_async_remote_copy(
+            src_ref=own_s, dst_ref=low_s, send_sem=ss_sem.at[0], recv_sem=sr_sem.at[0],
+            device_id={"member": up}, device_id_type=MESH,
+        )
+        to_down = pltpu.make_async_remote_copy(
+            src_ref=own_s, dst_ref=high_s, send_sem=ss_sem.at[1], recv_sem=sr_sem.at[1],
+            device_id={"member": down}, device_id_type=MESH,
+        )
+        return to_up, to_down
+
+    def share():
+        for s in range(SG):
+            own_s[s * 2 * mf : (s + 1) * 2 * mf, :] = spec_of(0, s)
+        for c in s_copies():
+            c.start()
+
+    def chosen_of(q, s):
+        out = []
+        for m in range(2):
+            chosen = None
+            for p in range(m, m + 2 * SPREAD + 1):
+                source = (low_s, own_s, high_s)[p // 2]
+                start = s * 2 * mf + (p % 2) * mf
+                cand = source[start : start + mf, :]
+                hit = jnp.broadcast_to(places[m] == p, cand.shape)
+                chosen = cand if chosen is None else jnp.where(hit, cand, chosen)
+            out.append(chosen)
+        return jnp.concatenate(out, axis=0)
+
+    forward(0)
+    share()
+    forward(1)
+    finish(1, spec_of)
+    for c in s_copies():
+        c.wait_recv()
+    finish(0, chosen_of)
+    for q in range(2, chunks):
+        forward(q)
+        finish(q, spec_of)
+
+    for c in s_copies():
+        c.wait_send()
     for q in range(chunks):
-        for c in x_copies(q):
-            c.wait_send()
+        if q > 0:
+            for h in range(halves):
+                for c in x_copies(q, h):
+                    c.wait_send()
         pltpu.make_async_remote_copy(
             src_ref=sel.at[q, pl.ds(0, lat_count - 1)], dst_ref=recv.at[q, pl.ds(0, lat_count - 1)],
-            send_sem=as_sem.at[q], recv_sem=ar_sem.at[q], device_id={"lat": me}, device_id_type=MESH,
+            send_sem=as_sem.at[q], recv_sem=ar_sem.at[q, 0], device_id={"lat": me}, device_id_type=MESH,
         ).wait_send()
         block = pl.ds(q * SG * 2 * mf, SG * 2 * mf)
         pltpu.make_async_copy(spec_v.at[block], spectra_out.at[block], out_sem.at[q, 0]).wait()
@@ -289,8 +411,6 @@
     out_rows = here * mem * 2 * fields
     chunk_rows = SG * 2 * mf
     any_spec = pl.BlockSpec(memory_space=pl.ANY)
-    smem = pl.BlockSpec(memory_space=pltpu.SMEM)
-    vmem = pl.BlockSpec(memory_space=pltpu.VMEM)
     msg = (chunks, lat_count, 2 * SG, rows)
     dma = pltpu.SemaphoreType.DMA
     spectra, fourier = pl.pallas_call(
@@ -299,14 +419,17 @@
             jax.ShapeDtypeStruct((out_rows, TRUNC), BF16),
             jax.ShapeDtypeStruct((out_rows, NLAT), BF16),
         ),
-        in_specs=[smem, smem, vmem, any_spec, any_spec, any_spec],
+        in_specs=[any_spec] * 6,
         out_specs=(any_spec, any_spec),
         scratch_shapes=[
+            pltpu.SMEM(parents.shape, jnp.int32),
+            pltpu.SMEM((slots,), jnp.int32),
+            pltpu.VMEM((slots // 128, 128), jnp.int32),
             pltpu.VMEM((slots, 128), F32),
             pltpu.VMEM((rows, lon), BF16),
             pltpu.VMEM((rows, lon), BF16),
             pltpu.VMEM((rows, lon), BF16),
-            pltpu.VMEM((lat_count * 2 * SG, lon), BF16),
+            pltpu.VMEM((lat_count // 2 * 2 * SG, lon), BF16),
             pltpu.VMEM(msg, BF16),
             pltpu.VMEM(msg, BF16),
             pltpu.VMEM(msg, BF16),
@@ -320,12 +443,18 @@
             pltpu.VMEM((out_rows, TRUNC), BF16),
             pltpu.VMEM((out_rows, TRUNC), BF16),
             pltpu.VMEM((out_rows, NLAT), BF16),
+            pltpu.VMEM((chunk_rows, NPAD), BF16),
+            pltpu.VMEM((chunk_rows, NPAD), BF16),
+            pltpu.VMEM((chunk_rows, NPAD), BF16),
+            dma((3,)),
+            dma((2,)),
+            dma((2,)),
             dma((2,)),
             dma,
-            dma((chunks, 2)),
-            dma((chunks, 2)),
+            dma((chunks, 2, 2)),
+            dma((chunks, 2, 2)),
             dma((chunks,)),
-            dma((chunks,)),
+            dma((chunks, lat_count * lat_local // 128)),
             dma((chunks, 2)),
         ],
         compiler_params=pltpu.CompilerParams(

time: 70.9 us -> 56.3 us (0.79)
  the two profiles are of different devices: /device:TPU:14 before, /device:TPU:1 now
where the time goes in v2:
time: 56.3 us; the launch traced here: 56.2 us
  Pallas kernels  52 us (92%)
  local copies, waits for them, and re-layouts  3.62 us (6%)
  between operations  0.65 us (1%)
    pallas_call x1, Pallas kernels, per_device(): pl.pallas_call(functools.partial(kernel, lat_count, member_count), out_sh...  52 us
    unnamed x4, local copies, waits for them, and re-layouts  3.62 us

profile of v2, /device:TPU:1, one launch (start us, length us, event | category | flops | bytes accessed | tf_op | source)
XLA Modules:
  0.0 56.2 jit_solution(10765727461923254025)
XLA Ops:
  0.6 52.0 %transform.1 = (bf16[768,683]{1,0:T(8,128)(2,1)}, bf16[768,1024]{1,0:T(8,128)(2,1)}) custom-call(s32[16]{0:T(128)} %parents_hbm.1, s32[768]{0:T(1024)} %waves_hbm.1, s32[6,128]{1,0:T(8,128)} %bitcast.11, bf16[512,2048]{1,0:T(8,128)(2,1)} %bitcast.6, bf16[512,2048]{1,0:T(8,128)(2,1)} %bitcast.7, bf16[768,683]{1,0:T(8,128)(2,1)} %bitcast.10), custom_call_target="tpu_custom_call" | custom-call | tf_op jit(solution)/shard_map/transform/pallas_call | solution.py:416
  52.6 0.0 copy-start
  52.6 2.5 %copy.9 = bf16[24,2,2,8,683]{4,3,2,1,0:T(8,128)(2,1)} copy(bf16[24,2,2,8,683]{4,3,2,1,0:T(8,128)(2,1)} %bitcast.9) | data formatting | bytes 2098176
  55.1 0.0 copy-done
  55.1 1.1 %copy.10 = bf16[24,2,2,8,1024]{4,3,2,1,0:T(8,128)(2,1)} copy(bf16[24,2,2,8,1024]{4,3,2,1,0:T(8,128)(2,1)S(1)} %bitcast.8) | data formatting | bytes 3145728
Async XLA Ops:
  52.6 2.5 %copy-start = (bf16[768,1024]{1,0:T(8,128)(2,1)S(1)}, bf16[768,1024]{1,0:T(8,128)(2,1)}, u32[]{:S(2)}) copy-start(bf16[768,1024]{1,0:T(8,128)(2,1)} %get-tuple-element.5) | copy-start | bytes 4718596

commit v3 on v2

--- a/solution.py
+++ b/solution.py
@@ -42,13 +42,63 @@
     return cos, sin
 
 
+def forward_rows(xmat, even_f, odd_f, wave, spec, mf):
+    w = wave.astype(jnp.int32)
+    fields = mf // 2
+    is_odd = (w & 1) == 1
+    x = xmat[...]
+    for nt in range(NPAD // 256):
+        cols = slice(256 * nt, 256 * nt + 256)
+        even = lax.dot_general(x, even_f[:, cols], NN, preferred_element_type=F32)
+        odd = lax.dot_general(x, odd_f[:, cols], NN, preferred_element_type=F32)
+        for half in range(2):
+            n = 256 * nt + 128 * half + iota((SG, 128), 1)
+            live = (n >= w) & (w < TRUNC) & (n < TRUNC)
+            lanes = slice(128 * half, 128 * half + 128)
+            for i in range(mf * 2):
+                member, field, part = i // (2 * fields), i // 2 % fields, i % 2
+                rows = slice(SG * i, SG * i + SG)
+                value = jnp.where(is_odd, odd[rows, lanes], even[rows, lanes])
+                value = jnp.where(live, value, 0.0)
+                start = member * 2 * fields + part * fields + field + (2 * nt + half) * SG * 2 * mf
+                spec[pl.ds(start, SG, stride=2 * mf), :] = value
+
+
+def spec_rows(spec, s, mf):
+    tiles = [spec[pl.ds((t * SG + s) * 2 * mf, 2 * mf), :] for t in range(NPAD // 128)]
+    return jnp.concatenate(tiles, axis=1).astype(BF16)
+
+
+def finish_rows(base_of, noise, even_t, odd_t, wave, kids, spec_out, four_out, mf):
+    w = wave.astype(jnp.int32)
+    wide = jnp.concatenate([w] * (NPAD // 128), axis=1)
+    for s in range(SG):
+        rows = slice(s * 2 * mf, (s + 1) * 2 * mf)
+        ws = wide[s : s + 1, :TRUNC]
+        live = (iota((2 * mf, TRUNC), 1) >= ws) & (ws < TRUNC)
+        base = base_of(s).astype(F32)[:, :TRUNC]
+        child = (base + jnp.where(live, noise[rows, :].astype(F32), 0.0)).astype(BF16)
+        spec_out[rows, :] = child
+        kids[rows, :TRUNC] = child
+        kids[rows, TRUNC:] = jnp.zeros((2 * mf, NPAD - TRUNC), BF16)
+    for nt in range(NLAT // 256):
+        cols = slice(256 * nt, 256 * nt + 256)
+        even = lax.dot_general(kids[...], even_t[:, cols], NN, preferred_element_type=F32)
+        odd = lax.dot_general(kids[...], odd_t[:, cols], NN, preferred_element_type=F32)
+        for s in range(SG):
+            rows = slice(s * 2 * mf, (s + 1) * 2 * mf)
+            ws = jnp.concatenate([w[s : s + 1, :]] * 2, axis=1)
+            is_odd = jnp.broadcast_to((ws & 1) == 1, (2 * mf, 256))
+            four_out[rows, cols] = jnp.where(is_odd, odd[rows], even[rows]).astype(BF16)
+
+
 def kernel(
     lat_count, member_count,
-    parents_hbm, waves_hbm, waves_row_hbm, velocity, tracer, noise,
-    spectra_out, fourier_out,
-    parents, waves, waves_row, wave_b, vel, tra, prod, table, four, low, high, sel, recv, even_t, odd_t,
-    xmat, spec, kids, noise_v, spec_v, four_v, own_s, low_s, high_s,
-    small_sem, ss_sem, sr_sem, in_sem, noise_sem, xs_sem, xr_sem, as_sem, ar_sem, out_sem,
+    parents_hbm, waves_row_hbm, velocity, tracer, noise,
+    spec_v, four_v, last_x, last_noise, last_wave, even_t, odd_t, even_f, odd_f,
+    parents, waves_row, wave_b, vel, tra, prod, table, four, low, high, sel, recv,
+    xmat, spec, kids, noise_v, own_s, low_s, high_s,
+    small_sem, ss_sem, sr_sem, in_sem, noise_sem, xs_sem, xr_sem, as_sem, ar_sem,
 ):
     me = lax.axis_index("lat")
     group = lax.axis_index("member")
@@ -58,11 +108,25 @@
     half_count = lat_count // halves
     lat_local = NLAT // lat_count
     mf = vel.shape[0] // lat_local
+    chunk_rows = SG * 2 * mf
     fields = mf // 2
 
     barrier = pltpu.get_barrier_semaphore()
     up = lax.rem(group + 1, member_count)
     down = lax.rem(group + member_count - 1, member_count)
+
+    pieces = 4
+    piece = vel.shape[0] // pieces
+
+    def loads(i):
+        block = pl.ds(i * piece, piece)
+        return (
+            pltpu.make_async_copy(velocity.at[block], vel.at[block], in_sem.at[0, i]),
+            pltpu.make_async_copy(tracer.at[block], tra.at[block], in_sem.at[1, i]),
+        )
+
+    for c in loads(0):
+        c.start()
 
     @pl.loop(1, lat_count)
     def _(o):
@@ -74,21 +138,13 @@
     pl.semaphore_signal(barrier, inc=1, device_id={"member": down}, device_id_type=MESH)
     load_w = pltpu.make_async_copy(waves_row_hbm, waves_row, small_sem.at[0])
     load_w.start()
-    load_v = pltpu.make_async_copy(velocity, vel, in_sem.at[0])
-    load_t = pltpu.make_async_copy(tracer, tra, in_sem.at[1])
-    load_v.start()
-    load_t.start()
-    load_s = pltpu.make_async_copy(waves_hbm, waves, small_sem.at[1])
-    load_s.start()
-    load_p = pltpu.make_async_copy(parents_hbm, parents, small_sem.at[2])
+    for i in range(1, pieces):
+        for c in loads(i):
+            c.start()
+    load_p = pltpu.make_async_copy(parents_hbm, parents, small_sem.at[1])
     load_p.start()
     load_n = pltpu.make_async_copy(noise, noise_v, noise_sem)
     load_n.start()
-    load_w.wait()
-
-    for r in range(waves_row.shape[0]):
-        row = waves_row[r : r + 1, :].astype(F32)
-        wave_b[128 * r : 128 * r + 128, :] = jnp.transpose(jnp.broadcast_to(row, (128, 128)))
 
     y_count = 128 // lat_local
     z_count = lat_count // y_count
@@ -142,13 +198,24 @@
         out = lax.dot_general(table[...], prod[...], NT, preferred_element_type=F32)
         four[q, first : first + half_count] = out.astype(BF16).reshape(half_count, 2 * SG, out.shape[1])
 
-    load_v.wait()
-    load_t.wait()
-
-    @pl.loop(0, vel.shape[0] // 16)
-    def _(b):
-        rows = pl.ds(pl.multiple_of(b * 16, 16), 16)
-        prod[rows, :] = (vel[rows, :].astype(F32) * tra[rows, :].astype(F32)).astype(BF16)
+    def make_waves():
+        load_w.wait()
+        for r in range(waves_row.shape[0]):
+            row = waves_row[r : r + 1, :].astype(F32)
+            wave_b[128 * r : 128 * r + 128, :] = jnp.transpose(jnp.broadcast_to(row, (128, 128)))
+
+    def make_product():
+        for i in range(pieces):
+            for c in loads(i):
+                c.wait()
+
+            @pl.loop(0, piece // 32)
+            def _(b):
+                rows = pl.ds(pl.multiple_of(i * piece + b * 32, 32), 32)
+                prod[rows, :] = (vel[rows, :].astype(F32) * tra[rows, :].astype(F32)).astype(BF16)
+
+    make_waves()
+    make_product()
 
     def x_copies(q, h):
         block = pl.ds(h * half_count, half_count)
@@ -190,33 +257,35 @@
             for c in x_copies(q, h):
                 c.start()
 
-    def make_basis():
+    def make_basis(even, odd, rows_are_degrees):
         step = 64
-        half_turn = 2 * NLAT
-        lanes = 128
-
-        @pl.loop(0, NLAT // lanes)
-        def _(jt):
-            j = jt * lanes + iota((8, lanes), 1)
+        period = 4 * NLAT
+        row_count, lane_count = even.shape
+        lanes = lane_count // (2 if rows_are_degrees else 3)
+        scale = math.sqrt(2.0 / NLAT)
+
+        @pl.loop(0, lane_count // lanes)
+        def _(tile):
+            lane = tile * lanes + iota((8, lanes), 1)
             sub = iota((8, lanes), 0)
-            c8, s8 = cos_sin((8 * (2 * j + 1)) & (2 * half_turn - 1), 2 * half_turn)
-            cols = pl.ds(pl.multiple_of(jt * lanes, lanes), lanes)
-            scale = math.sqrt(2.0 / NLAT)
-
-            @pl.loop(0, NPAD // step)
+            turn = 8 * (2 * lane + 1) if rows_are_degrees else 16 * lane
+            c8, s8 = cos_sin(turn & (period - 1), period)
+            cols = pl.ds(pl.multiple_of(tile * lanes, 128), lanes)
+
+            @pl.loop(0, row_count // step)
             def _(a):
-                n = a * step + sub
-                c, s = cos_sin((n * (2 * j + 1)) & (2 * half_turn - 1), 2 * half_turn)
+                row = a * step + sub
+                phase = row * (2 * lane + 1) if rows_are_degrees else lane * (2 * row + 1)
+                c, s = cos_sin(phase & (period - 1), period)
                 c = c * scale
                 s = s * scale
                 for b in range(step // 16):
                     c2, s2 = c * c8 - s * s8, s * c8 + c * s8
-                    n16 = pl.ds(pl.multiple_of(a * step + b * 16, 16), 16)
-                    even_t[n16, cols] = jnp.concatenate([c, c2], axis=0).astype(BF16)
-                    odd_t[n16, cols] = jnp.concatenate([s, s2], axis=0).astype(BF16)
+                    r16 = pl.ds(pl.multiple_of(a * step + b * 16, 16), 16)
+                    even[r16, cols] = jnp.concatenate([c, c2], axis=0).astype(BF16)
+                    odd[r16, cols] = jnp.concatenate([s, s2], axis=0).astype(BF16)
                     c, s = c2 * c8 - s2 * s8, s2 * c8 + c2 * s8
 
-    load_s.wait()
     load_p.wait()
     first_member = group * 2
     places = [parents[first_member + m] - first_member + SPREAD for m in range(2)]
@@ -245,9 +314,9 @@
         for h in range(halves):
             relay(q, h)
 
-    make_basis()
+    make_basis(even_f, odd_f, False)
+    make_basis(even_t, odd_t, True)
     load_n.wait()
-    kids[...] = jnp.zeros_like(kids)
 
     def arrive(q, p, count):
         block = recv.at[q, pl.ds(p * y_count, count)]
@@ -256,7 +325,7 @@
             device_id={"lat": me}, device_id_type=MESH,
         ).wait_recv()
 
-    def shuffle(q):
+    def shuffle(q, xmat):
         per = 128 // lat_local
         lane = iota((2 * SG, 128), 1) // lat_local
         low_half = lane < 2
@@ -288,61 +357,24 @@
         arrange(my_z)
 
     def forward(q):
-        shuffle(q)
+        shuffle(q, xmat)
         product(q)
 
+    def own_wave(q):
+        return wave_b[pl.ds(pl.multiple_of(me * slots_here + q * SG, SG), SG), :]
+
     def product(q):
-        w = wave_b[pl.ds(pl.multiple_of(me * slots_here + q * SG, SG), SG), :].astype(jnp.int32)
-        x = xmat[...]
-        for nt in range(NPAD // 256):
-            cols = slice(256 * nt, 256 * nt + 256)
-            even = lax.dot_general(x, even_t[cols, :], NT, preferred_element_type=F32)
-            odd = lax.dot_general(x, odd_t[cols, :], NT, preferred_element_type=F32)
-            for half in range(2):
-                n = 256 * nt + 128 * half + iota((SG, 128), 1)
-                live = (n >= w) & (w < TRUNC) & (n < TRUNC)
-                is_odd = (w & 1) == 1
-                lanes = slice(128 * half, 128 * half + 128)
-                for i in range(mf * 2):
-                    member, field, part = i // (2 * fields), i // 2 % fields, i % 2
-                    rows = slice(SG * i, SG * i + SG)
-                    value = jnp.where(is_odd, odd[rows, lanes], even[rows, lanes])
-                    value = jnp.where(live, value, 0.0)
-                    start = member * 2 * fields + part * fields + field
-                    start = start + (2 * nt + half) * SG * 2 * mf
-                    spec[pl.ds(start, SG, stride=2 * mf), :] = value
+        forward_rows(xmat, even_f, odd_f, own_wave(q), spec, mf)
 
     def finish(q, base_of):
-        for s in range(SG):
-            wave = waves[me * slots_here + q * SG + s]
-            rows = slice(s * 2 * mf, (s + 1) * 2 * mf)
-            out_rows = slice((q * SG + s) * 2 * mf, (q * SG + s + 1) * 2 * mf)
-            n = iota((2 * mf, TRUNC), 1)
-            live = (n >= wave) & (wave < TRUNC)
-            base = base_of(q, s).astype(F32)[:, :TRUNC]
-            extra = noise_v[out_rows, :].astype(F32)
-            child = (base + jnp.where(live, extra, 0.0)).astype(BF16)
-            spec_v[out_rows, :] = child
-            kids[rows, :TRUNC] = child
-
-        for nt in range(NLAT // 256):
-            cols = slice(256 * nt, 256 * nt + 256)
-            even = lax.dot_general(kids[...], even_t[:, cols], NN, preferred_element_type=F32)
-            odd = lax.dot_general(kids[...], odd_t[:, cols], NN, preferred_element_type=F32)
-            for s in range(SG):
-                wave = waves[me * slots_here + q * SG + s]
-                rows = slice(s * 2 * mf, (s + 1) * 2 * mf)
-                is_odd = jnp.broadcast_to((wave & 1) == 1, (2 * mf, 256))
-                value = jnp.where(is_odd, odd[rows], even[rows])
-                four_v[q * SG * 2 * mf + s * 2 * mf : q * SG * 2 * mf + (s + 1) * 2 * mf, cols] = value.astype(BF16)
-
-        block = pl.ds(q * SG * 2 * mf, SG * 2 * mf)
-        pltpu.make_async_copy(spec_v.at[block], spectra_out.at[block], out_sem.at[q, 0]).start()
-        pltpu.make_async_copy(four_v.at[block], fourier_out.at[block], out_sem.at[q, 1]).start()
-
-    def spec_of(q, s):
-        tiles = [spec[pl.ds((t * SG + s) * 2 * mf, 2 * mf), :] for t in range(NPAD // 128)]
-        return jnp.concatenate(tiles, axis=1).astype(BF16)
+        block = pl.ds(q * chunk_rows, chunk_rows)
+        finish_rows(
+            base_of, noise_v.at[block], even_t, odd_t, own_wave(q), kids,
+            spec_v.at[block], four_v.at[block], mf,
+        )
+
+    def own_of(s):
+        return spec_rows(spec, s, mf)
 
     def s_copies():
         to_up = pltpu.make_async_remote_copy(
@@ -357,11 +389,11 @@
 
     def share():
         for s in range(SG):
-            own_s[s * 2 * mf : (s + 1) * 2 * mf, :] = spec_of(0, s)
+            own_s[s * 2 * mf : (s + 1) * 2 * mf, :] = own_of(s)
         for c in s_copies():
             c.start()
 
-    def chosen_of(q, s):
+    def chosen_of(s):
         out = []
         for m in range(2):
             chosen = None
@@ -377,13 +409,13 @@
     forward(0)
     share()
     forward(1)
-    finish(1, spec_of)
+    finish(1, own_of)
     for c in s_copies():
         c.wait_recv()
     finish(0, chosen_of)
-    for q in range(2, chunks):
-        forward(q)
-        finish(q, spec_of)
+    last_noise[...] = noise_v[2 * chunk_rows : 3 * chunk_rows, :]
+    last_wave[...] = own_wave(2)
+    shuffle(2, last_x)
 
     for c in s_copies():
         c.wait_send()
@@ -396,9 +428,28 @@
             src_ref=sel.at[q, pl.ds(0, lat_count - 1)], dst_ref=recv.at[q, pl.ds(0, lat_count - 1)],
             send_sem=as_sem.at[q], recv_sem=ar_sem.at[q, 0], device_id={"lat": me}, device_id_type=MESH,
         ).wait_send()
-        block = pl.ds(q * SG * 2 * mf, SG * 2 * mf)
-        pltpu.make_async_copy(spec_v.at[block], spectra_out.at[block], out_sem.at[q, 0]).wait()
-        pltpu.make_async_copy(four_v.at[block], fourier_out.at[block], out_sem.at[q, 1]).wait()
+
+
+def tail(mf, spec_v, four_v, x, noise, wave, even_t, odd_t, even_f, odd_f, spectra_out, fourier_out, spec, kids, spec_l, four_l, sem):
+    done = spec_v.shape[0]
+    rows = x.shape[0]
+    early = (
+        pltpu.make_async_copy(spec_v, spectra_out.at[pl.ds(0, done)], sem.at[0]),
+        pltpu.make_async_copy(four_v, fourier_out.at[pl.ds(0, done)], sem.at[1]),
+    )
+    for c in early:
+        c.start()
+    w = wave[...]
+    forward_rows(x, even_f, odd_f, w, spec, mf)
+    finish_rows(lambda s: spec_rows(spec, s, mf), noise, even_t, odd_t, w, kids, spec_l, four_l, mf)
+    late = (
+        pltpu.make_async_copy(spec_l, spectra_out.at[pl.ds(done, rows)], sem.at[2]),
+        pltpu.make_async_copy(four_l, fourier_out.at[pl.ds(done, rows)], sem.at[3]),
+    )
+    for c in late:
+        c.start()
+    for c in early + late:
+        c.wait()
 
 
 def per_device(lat_count, member_count, velocity, tracer, wave_slots, parents, noise):
@@ -410,20 +461,29 @@
     mf = mem * fields
     out_rows = here * mem * 2 * fields
     chunk_rows = SG * 2 * mf
-    any_spec = pl.BlockSpec(memory_space=pl.ANY)
     msg = (chunks, lat_count, 2 * SG, rows)
     dma = pltpu.SemaphoreType.DMA
-    spectra, fourier = pl.pallas_call(
+    hbm = pl.BlockSpec(memory_space=pltpu.HBM)
+    vmem = pl.BlockSpec(memory_space=pltpu.VMEM)
+    early = out_rows - chunk_rows
+    middle = (
+        jax.ShapeDtypeStruct((early, TRUNC), BF16),
+        jax.ShapeDtypeStruct((early, NLAT), BF16),
+        jax.ShapeDtypeStruct((chunk_rows, NLAT), BF16),
+        jax.ShapeDtypeStruct((chunk_rows, TRUNC), BF16),
+        jax.ShapeDtypeStruct((SG, 128), F32),
+        jax.ShapeDtypeStruct((NPAD, NLAT), BF16),
+        jax.ShapeDtypeStruct((NPAD, NLAT), BF16),
+        jax.ShapeDtypeStruct((NLAT, NPAD), BF16),
+        jax.ShapeDtypeStruct((NLAT, NPAD), BF16),
+    )
+    parts = pl.pallas_call(
         functools.partial(kernel, lat_count, member_count),
-        out_shape=(
-            jax.ShapeDtypeStruct((out_rows, TRUNC), BF16),
-            jax.ShapeDtypeStruct((out_rows, NLAT), BF16),
-        ),
-        in_specs=[any_spec] * 6,
-        out_specs=(any_spec, any_spec),
+        out_shape=middle,
+        in_specs=[hbm] * 5,
+        out_specs=(vmem,) * len(middle),
         scratch_shapes=[
             pltpu.SMEM(parents.shape, jnp.int32),
-            pltpu.SMEM((slots,), jnp.int32),
             pltpu.VMEM((slots // 128, 128), jnp.int32),
             pltpu.VMEM((slots, 128), F32),
             pltpu.VMEM((rows, lon), BF16),
@@ -435,40 +495,52 @@
             pltpu.VMEM(msg, BF16),
             pltpu.VMEM(msg, BF16),
             pltpu.VMEM(msg, BF16),
-            pltpu.VMEM((NPAD, NLAT), BF16),
-            pltpu.VMEM((NPAD, NLAT), BF16),
             pltpu.VMEM((chunk_rows, NLAT), BF16),
             pltpu.VMEM((NPAD // 128 * chunk_rows, 128), F32),
             pltpu.VMEM((chunk_rows, NPAD), BF16),
             pltpu.VMEM((out_rows, TRUNC), BF16),
-            pltpu.VMEM((out_rows, TRUNC), BF16),
-            pltpu.VMEM((out_rows, NLAT), BF16),
             pltpu.VMEM((chunk_rows, NPAD), BF16),
             pltpu.VMEM((chunk_rows, NPAD), BF16),
             pltpu.VMEM((chunk_rows, NPAD), BF16),
-            dma((3,)),
             dma((2,)),
             dma((2,)),
             dma((2,)),
+            dma((2, 4)),
             dma,
             dma((chunks, 2, 2)),
             dma((chunks, 2, 2)),
             dma((chunks,)),
             dma((chunks, lat_count * lat_local // 128)),
-            dma((chunks, 2)),
         ],
         compiler_params=pltpu.CompilerParams(
-            collective_id=0, has_side_effects=True, vmem_limit_bytes=60 * 1024 * 1024
+            collective_id=0, has_side_effects=True, vmem_limit_bytes=44 * 1024 * 1024
         ),
         name="transform",
     )(
-        parents,
-        wave_slots,
-        wave_slots.reshape(slots // 128, 128),
-        velocity.reshape(rows, lon),
-        tracer.reshape(rows, lon),
-        noise.reshape(out_rows, TRUNC),
-    )
+        pltpu.with_memory_space_constraint(parents, pltpu.HBM),
+        pltpu.with_memory_space_constraint(wave_slots.reshape(slots // 128, 128), pltpu.HBM),
+        pltpu.with_memory_space_constraint(velocity.reshape(rows, lon), pltpu.HBM),
+        pltpu.with_memory_space_constraint(tracer.reshape(rows, lon), pltpu.HBM),
+        pltpu.with_memory_space_constraint(noise.reshape(out_rows, TRUNC), pltpu.HBM),
+    )
+    spectra, fourier = pl.pallas_call(
+        functools.partial(tail, mf),
+        out_shape=(
+            jax.ShapeDtypeStruct((out_rows, TRUNC), BF16),
+            jax.ShapeDtypeStruct((out_rows, NLAT), BF16),
+        ),
+        in_specs=[vmem] * len(middle),
+        out_specs=(hbm, hbm),
+        scratch_shapes=[
+            pltpu.VMEM((NPAD // 128 * chunk_rows, 128), F32),
+            pltpu.VMEM((chunk_rows, NPAD), BF16),
+            pltpu.VMEM((chunk_rows, TRUNC), BF16),
+            pltpu.VMEM((chunk_rows, NLAT), BF16),
+            dma((4,)),
+        ],
+        compiler_params=pltpu.CompilerParams(vmem_limit_bytes=44 * 1024 * 1024),
+        name="last",
+    )(*parts)
     return (
         spectra.reshape(here, mem, 2, fields, TRUNC),
         fourier.reshape(here, mem, 2, fields, NLAT),

time: 56.3 us -> 52 us (0.924)
  local copies, waits for them, and re-layouts: 3.62 us -> 0 us
  Pallas kernels: 52 us -> 51.2 us
    pallas_call x1, Pallas kernels: 52 us -> 47.9 us  [per_device(): pl.pallas_call(functools.partial(kernel, lat_count, member_count), out_sh...]
    unnamed x4 -> x0, local copies, waits for them, and re-layouts: 3.62 us -> none
    pallas_call x0 -> x1, Pallas kernels: none -> 3.32 us  [per_device(): pl.pallas_call(functools.partial(tail, mf), out_shape=(jax.ShapeDtypeStru...]
where the time goes in v3:
time: 52 us; the launch traced here: 51.9 us
  Pallas kernels  51.2 us (98%)
  between operations  0.64 us (1%)
    pallas_call x1, Pallas kernels, per_device(): pl.pallas_call(functools.partial(kernel, lat_count, member_count), out_sh...  47.9 us
    pallas_call x1, Pallas kernels, per_device(): pl.pallas_call(functools.partial(tail, mf), out_shape=(jax.ShapeDtypeStru...  3.32 us

profile of v3, /device:TPU:1, one launch (start us, length us, event | category | flops | bytes accessed | tf_op | source)
XLA Modules:
  0.0 51.9 jit_solution(16804793877296706463)
XLA Ops:
  0.6 47.9 %transform.1 = (bf16[512,683]{1,0:T(8,128)(2,1)S(1)}, bf16[512,1024]{1,0:T(8,128)(2,1)S(1)}, bf16[256,1024]{1,0:T(8,128)(2,1)S(1)}, bf16[256,683]{1,0:T(8,128)(2...) custom-call(s32[16]{0:T(128)} %parents_hbm.1, ...), custom_call_target="tpu_custom_call" | custom-call | tf_op jit(solution)/shard_map/transform/pallas_call | solution.py:480
  48.6 3.3 %last.1 = (bf16[768,683]{1,0:T(8,128)(2,1)}, bf16[768,1024]{1,0:T(8,128)(2,1)}) custom-call(bf16[512,683]{1,0:T(8,128)(2,1)S(1)} %get-tuple-element.13.spec_v, bf16[512,1024]{1,0:T(8,128)(2,1)S(1)} %get-tuple-element.14.four_v, bf16[256,1024]{1,0:T(8,128)(2,1)S(1)} %get-tuple-element.15.x, bf16[256,683]{1,0:T(8,128)(2,1)S(1)} %get-tuple-element.16.noise, ...), custom_call_target="tpu_custom_call" | custom-call | tf_op jit(solution)/shard_map/last/pallas_call | solution.py:526

commit v4 on v3

--- a/solution.py
+++ b/solution.py
@@ -42,34 +42,44 @@
     return cos, sin
 
 
-def forward_rows(xmat, even_f, odd_f, wave, spec, mf):
-    w = wave.astype(jnp.int32)
-    fields = mf // 2
-    is_odd = (w & 1) == 1
-    x = xmat[...]
+def by_parity(x, even_f, odd_f, cols, is_odd):
+    even = lax.dot_general(x, even_f[:, cols], NN, preferred_element_type=F32)
+    odd = lax.dot_general(x, odd_f[:, cols], NN, preferred_element_type=F32)
+    out = []
+    for half in range(2):
+        lanes = slice(128 * half, 128 * half + 128)
+        groups = range(0, x.shape[0], SG)
+        out.append([jnp.where(is_odd, odd[i : i + SG, lanes], even[i : i + SG, lanes]) for i in groups])
+    return out
+
+
+def partial_rows(x, even_f, odd_f, wave, acc):
+    is_odd = (wave.astype(jnp.int32) & 1) == 1
     for nt in range(NPAD // 256):
         cols = slice(256 * nt, 256 * nt + 256)
-        even = lax.dot_general(x, even_f[:, cols], NN, preferred_element_type=F32)
-        odd = lax.dot_general(x, odd_f[:, cols], NN, preferred_element_type=F32)
-        for half in range(2):
-            n = 256 * nt + 128 * half + iota((SG, 128), 1)
+        for half, groups in enumerate(by_parity(x, even_f, odd_f, cols, is_odd)):
+            start = 256 * nt + 128 * half
+            acc[:, start : start + 128] = jnp.concatenate(groups, axis=0)
+
+
+def forward_rows(x, even_f, odd_f, wave, order, acc, spec):
+    w = wave.astype(jnp.int32)
+    is_odd = (w & 1) == 1
+    for nt in range(NPAD // 256):
+        cols = slice(256 * nt, 256 * nt + 256)
+        tiles = []
+        for half, groups in enumerate(by_parity(x, even_f, odd_f, cols, is_odd)):
+            start = 256 * nt + 128 * half
+            n = start + iota((SG, 128), 1)
             live = (n >= w) & (w < TRUNC) & (n < TRUNC)
-            lanes = slice(128 * half, 128 * half + 128)
-            for i in range(mf * 2):
-                member, field, part = i // (2 * fields), i // 2 % fields, i % 2
-                rows = slice(SG * i, SG * i + SG)
-                value = jnp.where(is_odd, odd[rows, lanes], even[rows, lanes])
-                value = jnp.where(live, value, 0.0)
-                start = member * 2 * fields + part * fields + field + (2 * nt + half) * SG * 2 * mf
-                spec[pl.ds(start, SG, stride=2 * mf), :] = value
-
-
-def spec_rows(spec, s, mf):
-    tiles = [spec[pl.ds((t * SG + s) * 2 * mf, 2 * mf), :] for t in range(NPAD // 128)]
-    return jnp.concatenate(tiles, axis=1).astype(BF16)
-
-
-def finish_rows(base_of, noise, even_t, odd_t, wave, kids, spec_out, four_out, mf):
+            if acc is not None:
+                groups = [g + acc[SG * i : SG * i + SG, start : start + 128] for i, g in enumerate(groups)]
+            tiles.append(jnp.concatenate([jnp.where(live, g, 0.0) for g in groups], axis=0))
+        value = jnp.concatenate(tiles, axis=1).astype(BF16)
+        spec[:, cols] = lax.dot_general(order, value, NN, preferred_element_type=F32).astype(BF16)
+
+
+def finish_rows(base_of, noise, even_t, odd_t, wave, kids, spec_out, four_out, mf, ready=lambda part: None):
     w = wave.astype(jnp.int32)
     wide = jnp.concatenate([w] * (NPAD // 128), axis=1)
     for s in range(SG):
@@ -81,6 +91,7 @@
         spec_out[rows, :] = child
         kids[rows, :TRUNC] = child
         kids[rows, TRUNC:] = jnp.zeros((2 * mf, NPAD - TRUNC), BF16)
+    ready(0)
     for nt in range(NLAT // 256):
         cols = slice(256 * nt, 256 * nt + 256)
         even = lax.dot_general(kids[...], even_t[:, cols], NN, preferred_element_type=F32)
@@ -90,14 +101,15 @@
             ws = jnp.concatenate([w[s : s + 1, :]] * 2, axis=1)
             is_odd = jnp.broadcast_to((ws & 1) == 1, (2 * mf, 256))
             four_out[rows, cols] = jnp.where(is_odd, odd[rows], even[rows]).astype(BF16)
+        ready(nt + 1)
 
 
 def kernel(
     lat_count, member_count,
     parents_hbm, waves_row_hbm, velocity, tracer, noise,
-    spec_v, four_v, last_x, last_noise, last_wave, even_t, odd_t, even_f, odd_f,
+    spec_v, four_v, acc, last_x, last_noise, last_wave, order, even_t, odd_t, even_l, odd_l,
     parents, waves_row, wave_b, vel, tra, prod, table, four, low, high, sel, recv,
-    xmat, spec, kids, noise_v, own_s, low_s, high_s,
+    even_f, odd_f, xmat, spec, kids, noise_v, own_s, low_s, high_s,
     small_sem, ss_sem, sr_sem, in_sem, noise_sem, xs_sem, xr_sem, as_sem, ar_sem,
 ):
     me = lax.axis_index("lat")
@@ -154,9 +166,13 @@
         r = z_count - 1 - k
         return (r + 1) // 2 * (1 - 2 * lax.rem(r + 1, 2))
 
-    def target_of(i):
-        z = lax.rem(my_z + turn_of(i // y_count) + z_count, z_count)
-        return z * y_count + lax.rem(my_y + i + 1, y_count)
+    def target_of(q, i):
+        if q < chunks - 1:
+            k, y = lax.rem(i, z_count), i // z_count + 1
+        else:
+            k, y = i // y_count, i + 1
+        z = lax.rem(my_z + turn_of(k) + z_count, z_count)
+        return z * y_count + lax.rem(my_y + y, y_count)
 
     def make_table(q, first):
         together = 4
@@ -166,7 +182,7 @@
             w = jnp.concatenate(
                 [
                     wave_b[
-                        pl.ds(pl.multiple_of(target_of(first + b * together + j) * slots_here + q * SG, SG), SG), :
+                        pl.ds(pl.multiple_of(target_of(q, first + b * together + j) * slots_here + q * SG, SG), SG), :
                     ]
                     for j in range(together)
                 ],
@@ -240,7 +256,7 @@
             pltpu.make_async_remote_copy(
                 src_ref=source.at[q, i], dst_ref=recv.at[q, me],
                 send_sem=as_sem.at[q], recv_sem=ar_sem.at[q, my_z],
-                device_id={"lat": target_of(i)}, device_id_type=MESH,
+                device_id={"lat": target_of(q, i)}, device_id_type=MESH,
             ).start()
 
         if last:
@@ -257,6 +273,16 @@
             for c in x_copies(q, h):
                 c.start()
 
+    def source_of(k):
+        return lax.rem(my_z - turn_of(k) + z_count, z_count)
+
+    def make_order():
+        row = iota(order.shape, 0)
+        col = iota(order.shape, 1)
+        slot, member, part, field = row // (2 * mf), row // mf % 2, row // fields % 2, row % fields
+        source = ((member * fields + field) * 2 + part) * SG + slot
+        order[...] = jnp.where(col == source, 1.0, 0.0).astype(BF16)
+
     def make_basis(even, odd, rows_are_degrees):
         step = 64
         period = 4 * NLAT
@@ -275,6 +301,8 @@
             @pl.loop(0, row_count // step)
             def _(a):
                 row = a * step + sub
+                if not rows_are_degrees:
+                    row = row + (source_of(a // 2) - a // 2) * 128
                 phase = row * (2 * lane + 1) if rows_are_degrees else lane * (2 * row + 1)
                 c, s = cos_sin(phase & (period - 1), period)
                 c = c * scale
@@ -310,12 +338,14 @@
         select_half(q, h)
         send_half(q, h, sel)
 
-    for q in range(1, chunks):
-        for h in range(halves):
-            relay(q, h)
-
+    relay(1, 0)
     make_basis(even_f, odd_f, False)
+    relay(1, 1)
     make_basis(even_t, odd_t, True)
+    relay(2, 0)
+    make_order()
+    relay(2, 1)
+
     load_n.wait()
 
     def arrive(q, p, count):
@@ -325,7 +355,9 @@
             device_id={"lat": me}, device_id_type=MESH,
         ).wait_recv()
 
-    def shuffle(q, xmat):
+    split = z_count - 2
+
+    def shuffle(q, begin, end):
         per = 128 // lat_local
         lane = iota((2 * SG, 128), 1) // lat_local
         low_half = lane < 2
@@ -336,35 +368,36 @@
             right = jnp.where(mask, pltpu.roll(x, 128 - width, 1), y)
             return left, right
 
-        def arrange(p):
-            target = pl.ds(pl.multiple_of(p * 128, 128), 128)
+        def arrange(p, k):
+            target = pl.ds(pl.multiple_of(k * 128, 128), 128)
             for t in range(mf // per):
                 x0, x1, x2, x3 = [recv[q, p * per + i, :, 128 * t : 128 * t + 128] for i in range(per)]
                 x0, x2 = swap(x0, x2, low_half, 2 * lat_local)
                 x1, x3 = swap(x1, x3, low_half, 2 * lat_local)
                 x0, x1 = swap(x0, x1, even_block, lat_local)
                 x2, x3 = swap(x2, x3, even_block, lat_local)
-                for k, x in enumerate((x0, x1, x2, x3)):
-                    xmat[(t * per + k) * 2 * SG : (t * per + k + 1) * 2 * SG, target] = x
-
-        @pl.loop(0, z_count - 1)
+                for j, x in enumerate((x0, x1, x2, x3)):
+                    xmat[(t * per + j) * 2 * SG : (t * per + j + 1) * 2 * SG, target] = x
+
+        @pl.loop(begin, min(end, z_count - 1))
         def _(k):
-            p = lax.rem(my_z - turn_of(k) + z_count, z_count)
+            p = source_of(k)
             arrive(q, p, per)
-            arrange(p)
-
-        arrive(q, my_z, per - 1)
-        arrange(my_z)
+            arrange(p, k)
+
+        if end == z_count:
+            arrive(q, my_z, per - 1)
+            arrange(my_z, z_count - 1)
 
     def forward(q):
-        shuffle(q, xmat)
+        shuffle(q, 0, z_count)
         product(q)
 
     def own_wave(q):
         return wave_b[pl.ds(pl.multiple_of(me * slots_here + q * SG, SG), SG), :]
 
     def product(q):
-        forward_rows(xmat, even_f, odd_f, own_wave(q), spec, mf)
+        forward_rows(xmat[...], even_f, odd_f, own_wave(q), order[...], None, spec)
 
     def finish(q, base_of):
         block = pl.ds(q * chunk_rows, chunk_rows)
@@ -374,7 +407,7 @@
         )
 
     def own_of(s):
-        return spec_rows(spec, s, mf)
+        return spec[s * 2 * mf : (s + 1) * 2 * mf, :]
 
     def s_copies():
         to_up = pltpu.make_async_remote_copy(
@@ -415,7 +448,13 @@
     finish(0, chosen_of)
     last_noise[...] = noise_v[2 * chunk_rows : 3 * chunk_rows, :]
     last_wave[...] = own_wave(2)
-    shuffle(2, last_x)
+    even_l[...] = even_f[split * 128 :, :]
+    odd_l[...] = odd_f[split * 128 :, :]
+    shuffle(2, 0, split)
+    early = pl.ds(0, split * 128)
+    partial_rows(xmat[:, :split * 128], even_f.at[early], odd_f.at[early], own_wave(2), acc)
+    shuffle(2, split, z_count)
+    last_x[...] = xmat[:, split * 128 :]
 
     for c in s_copies():
         c.wait_send()
@@ -430,25 +469,34 @@
         ).wait_send()
 
 
-def tail(mf, spec_v, four_v, x, noise, wave, even_t, odd_t, even_f, odd_f, spectra_out, fourier_out, spec, kids, spec_l, four_l, sem):
+def tail(
+    mf, spec_v, four_v, acc, x, noise, wave, order, even_t, odd_t, even_l, odd_l,
+    spectra_out, fourier_out, spec, kids, spec_l, four_l, sem,
+):
     done = spec_v.shape[0]
     rows = x.shape[0]
-    early = (
+    copies = [
         pltpu.make_async_copy(spec_v, spectra_out.at[pl.ds(0, done)], sem.at[0]),
         pltpu.make_async_copy(four_v, fourier_out.at[pl.ds(0, done)], sem.at[1]),
-    )
-    for c in early:
+    ]
+    for c in copies:
         c.start()
     w = wave[...]
-    forward_rows(x, even_f, odd_f, w, spec, mf)
-    finish_rows(lambda s: spec_rows(spec, s, mf), noise, even_t, odd_t, w, kids, spec_l, four_l, mf)
-    late = (
-        pltpu.make_async_copy(spec_l, spectra_out.at[pl.ds(done, rows)], sem.at[2]),
-        pltpu.make_async_copy(four_l, fourier_out.at[pl.ds(done, rows)], sem.at[3]),
+    forward_rows(x[...], even_l, odd_l, w, order[...], acc, spec)
+
+    def ready(part):
+        if part == 0:
+            c = pltpu.make_async_copy(spec_l, spectra_out.at[pl.ds(done, rows)], sem.at[2])
+        else:
+            cols = pl.ds(256 * (part - 1), 256)
+            c = pltpu.make_async_copy(four_l.at[:, cols], fourier_out.at[pl.ds(done, rows), cols], sem.at[2 + part])
+        copies.append(c)
+        c.start()
+
+    finish_rows(
+        lambda s: spec[s * 2 * mf : (s + 1) * 2 * mf, :], noise, even_t, odd_t, w, kids, spec_l, four_l, mf, ready
     )
-    for c in late:
-        c.start()
-    for c in early + late:
+    for c in copies:
         c.wait()
 
 
@@ -469,13 +517,15 @@
     middle = (
         jax.ShapeDtypeStruct((early, TRUNC), BF16),
         jax.ShapeDtypeStruct((early, NLAT), BF16),
-        jax.ShapeDtypeStruct((chunk_rows, NLAT), BF16),
+        jax.ShapeDtypeStruct((chunk_rows, NPAD), F32),
+        jax.ShapeDtypeStruct((chunk_rows, 256), BF16),
         jax.ShapeDtypeStruct((chunk_rows, TRUNC), BF16),
         jax.ShapeDtypeStruct((SG, 128), F32),
+        jax.ShapeDtypeStruct((chunk_rows, chunk_rows), BF16),
         jax.ShapeDtypeStruct((NPAD, NLAT), BF16),
         jax.ShapeDtypeStruct((NPAD, NLAT), BF16),
-        jax.ShapeDtypeStruct((NLAT, NPAD), BF16),
-        jax.ShapeDtypeStruct((NLAT, NPAD), BF16),
+        jax.ShapeDtypeStruct((256, NPAD), BF16),
+        jax.ShapeDtypeStruct((256, NPAD), BF16),
     )
     parts = pl.pallas_call(
         functools.partial(kernel, lat_count, member_count),
@@ -495,8 +545,10 @@
             pltpu.VMEM(msg, BF16),
             pltpu.VMEM(msg, BF16),
             pltpu.VMEM(msg, BF16),
+            pltpu.VMEM((NLAT, NPAD), BF16),
+            pltpu.VMEM((NLAT, NPAD), BF16),
             pltpu.VMEM((chunk_rows, NLAT), BF16),
-            pltpu.VMEM((NPAD // 128 * chunk_rows, 128), F32),
+            pltpu.VMEM((chunk_rows, NPAD), BF16),
             pltpu.VMEM((chunk_rows, NPAD), BF16),
             pltpu.VMEM((out_rows, TRUNC), BF16),
             pltpu.VMEM((chunk_rows, NPAD), BF16),
@@ -532,11 +584,11 @@
         in_specs=[vmem] * len(middle),
         out_specs=(hbm, hbm),
         scratch_shapes=[
-            pltpu.VMEM((NPAD // 128 * chunk_rows, 128), F32),
+            pltpu.VMEM((chunk_rows, NPAD), BF16),
             pltpu.VMEM((chunk_rows, NPAD), BF16),
             pltpu.VMEM((chunk_rows, TRUNC), BF16),
             pltpu.VMEM((chunk_rows, NLAT), BF16),
-            dma((4,)),
+            dma((3 + NLAT // 256,)),
         ],
         compiler_params=pltpu.CompilerParams(vmem_limit_bytes=44 * 1024 * 1024),
         name="last",

time: 52 us -> 51 us (0.981)
  Pallas kernels: 51.2 us -> 50.2 us
    pallas_call x1, Pallas kernels: 3.32 us -> 2.59 us  [per_device(): pl.pallas_call(functools.partial(tail, mf), out_shape=(jax.ShapeDtypeStru...]
where the time goes in v4:
time: 51 us; the launch traced here: 50.9 us
  Pallas kernels  50.2 us (98%)
  between operations  0.64 us (1%)
    pallas_call x1, Pallas kernels, per_device(): pl.pallas_call(functools.partial(kernel, lat_count, member_count), out_sh...  47.7 us
    pallas_call x1, Pallas kernels, per_device(): pl.pallas_call(functools.partial(tail, mf), out_shape=(jax.ShapeDtypeStru...  2.59 us

profile of v4, /device:TPU:1, one launch (start us, length us, event | category | flops | bytes accessed | tf_op | source)
XLA Modules:
  0.0 50.9 jit_solution(2602808081743107093)
XLA Ops:
  0.6 47.7 %transform.1 = (bf16[512,683]{1,0:T(8,128)(2,1)S(1)}, bf16[512,1024]{1,0:T(8,128)(2,1)S(1)}, f32[256,768]{1,0:T(8,128)S(1)}, bf16[256,256]{1,0:T(8,128)(2,1)S(1)...) custom-call(s32[16]{0:T(128)} %parents_hbm.1, ...), custom_call_target="tpu_custom_call" | custom-call | tf_op jit(solution)/shard_map/transform/pallas_call | solution.py:530
  48.3 2.6 %last.1 = (bf16[768,683]{1,0:T(8,128)(2,1)}, bf16[768,1024]{1,0:T(8,128)(2,1)}) custom-call(bf16[512,683]{1,0:T(8,128)(2,1)S(1)} %get-tuple-element.15.spec_v, bf16[512,1024]{1,0:T(8,128)(2,1)S(1)} %get-tuple-element.16.four_v, f32[256,768]{1,0:T(8,128)S(1)} %get-tuple-element.17.acc, bf16[256,256]{1,0:T(8,128)(2,1)S(1)} %get-tuple-element.18.x, ...), custom_call_target="tpu_custom_call" | custom-call | tf_op jit(solution)/shard_map/last/pallas_call | solution.py:578

commit v5 on v4

--- a/solution.py
+++ b/solution.py
@@ -140,8 +140,7 @@
     for c in loads(0):
         c.start()
 
-    @pl.loop(1, lat_count)
-    def _(o):
+    for o in sorted(range(1, lat_count), key=lambda o: abs(o - lat_count // 2)):
         pl.semaphore_signal(
             barrier, inc=1, device_id={"lat": lax.rem(me + o, lat_count)}, device_id_type=MESH
         )

time: 51 us -> 50.8 us (level)
  no operation moved by 1% of the time
where the time goes in v5:
time: 50.8 us; the launch traced here: 50.7 us
  Pallas kernels  50.1 us (99%)
  between operations  0.64 us (1%)
    pallas_call x1, Pallas kernels, per_device(): pl.pallas_call(functools.partial(kernel, lat_count, member_count), out_sh...  47.5 us
    pallas_call x1, Pallas kernels, per_device(): pl.pallas_call(functools.partial(tail, mf), out_shape=(jax.ShapeDtypeStru...  2.59 us

profile of v5, /device:TPU:1, one launch (start us, length us, event | category | flops | bytes accessed | tf_op | source)
XLA Modules:
  0.0 50.7 jit_solution(582156324773011138)
XLA Ops:
  0.6 47.5 %transform.1 = (bf16[512,683]{1,0:T(8,128)(2,1)S(1)}, bf16[512,1024]{1,0:T(8,128)(2,1)S(1)}, f32[256,768]{1,0:T(8,128)S(1)}, bf16[256,256]{1,0:T(8,128)(2,1)S(1)...) custom-call(s32[16]{0:T(128)} %parents_hbm.1, ...), custom_call_target="tpu_custom_call" | custom-call | tf_op jit(solution)/shard_map/transform/pallas_call | solution.py:529
  48.1 2.6 %last.1 = (bf16[768,683]{1,0:T(8,128)(2,1)}, bf16[768,1024]{1,0:T(8,128)(2,1)}) custom-call(bf16[512,683]{1,0:T(8,128)(2,1)S(1)} %get-tuple-element.15.spec_v, bf16[512,1024]{1,0:T(8,128)(2,1)S(1)} %get-tuple-element.16.four_v, f32[256,768]{1,0:T(8,128)S(1)} %get-tuple-element.17.acc, bf16[256,256]{1,0:T(8,128)(2,1)S(1)} %get-tuple-element.18.x, ...), custom_call_target="tpu_custom_call" | custom-call | tf_op jit(solution)/shard_map/last/pallas_call | solution.py:577

commit v6 on v5

--- a/solution.py
+++ b/solution.py
@@ -264,13 +264,18 @@
     zonal(0, 0)
     pl.semaphore_wait(barrier, lat_count + 1)
     send_half(0, 0, four)
+    def coefficients(q, h):
+        zonal(q, h)
+        for c in x_copies(q, h):
+            c.start()
+
+    coefficients(1, 0)
     zonal(0, 1)
     send_half(0, 1, four)
-    for q in range(1, chunks):
+    coefficients(1, 1)
+    for q in range(2, chunks):
         for h in range(halves):
-            zonal(q, h)
-            for c in x_copies(q, h):
-                c.start()
+            coefficients(q, h)
 
     def source_of(k):
         return lax.rem(my_z - turn_of(k) + z_count, z_count)
@@ -338,12 +343,12 @@
         send_half(q, h, sel)
 
     relay(1, 0)
+    relay(1, 1)
     make_basis(even_f, odd_f, False)
-    relay(1, 1)
-    make_basis(even_t, odd_t, True)
     relay(2, 0)
     make_order()
     relay(2, 1)
+    make_basis(even_t, odd_t, True)
 
     load_n.wait()
 
@@ -356,7 +361,7 @@
 
     split = z_count - 2
 
-    def shuffle(q, begin, end):
+    def shuffle(q, begin, end, out=xmat, shift=0):
         per = 128 // lat_local
         lane = iota((2 * SG, 128), 1) // lat_local
         low_half = lane < 2
@@ -368,7 +373,7 @@
             return left, right
 
         def arrange(p, k):
-            target = pl.ds(pl.multiple_of(k * 128, 128), 128)
+            target = pl.ds(pl.multiple_of((k - shift) * 128, 128), 128)
             for t in range(mf // per):
                 x0, x1, x2, x3 = [recv[q, p * per + i, :, 128 * t : 128 * t + 128] for i in range(per)]
                 x0, x2 = swap(x0, x2, low_half, 2 * lat_local)
@@ -376,7 +381,7 @@
                 x0, x1 = swap(x0, x1, even_block, lat_local)
                 x2, x3 = swap(x2, x3, even_block, lat_local)
                 for j, x in enumerate((x0, x1, x2, x3)):
-                    xmat[(t * per + j) * 2 * SG : (t * per + j + 1) * 2 * SG, target] = x
+                    out[(t * per + j) * 2 * SG : (t * per + j + 1) * 2 * SG, target] = x
 
         @pl.loop(begin, min(end, z_count - 1))
         def _(k):
@@ -452,8 +457,7 @@
     shuffle(2, 0, split)
     early = pl.ds(0, split * 128)
     partial_rows(xmat[:, :split * 128], even_f.at[early], odd_f.at[early], own_wave(2), acc)
-    shuffle(2, split, z_count)
-    last_x[...] = xmat[:, split * 128 :]
+    shuffle(2, split, z_count, last_x, split)
 
     for c in s_copies():
         c.wait_send()

time: 50.8 us -> 50.8 us (level)
  no operation moved by 1% of the time
where the time goes in v6:
time: 50.8 us; the launch traced here: 50.6 us
  Pallas kernels  50 us (98%)
  between operations  0.64 us (1%)
    pallas_call x1, Pallas kernels, per_device(): pl.pallas_call(functools.partial(kernel, lat_count, member_count), out_sh...  47.4 us
    pallas_call x1, Pallas kernels, per_device(): pl.pallas_call(functools.partial(tail, mf), out_shape=(jax.ShapeDtypeStru...  2.59 us

profile of v6, /device:TPU:1, one launch (start us, length us, event | category | flops | bytes accessed | tf_op | source)
XLA Modules:
  0.0 50.6 jit_solution(7760943515980748734)
XLA Ops:
  0.6 47.4 %transform.1 = (bf16[512,683]{1,0:T(8,128)(2,1)S(1)}, bf16[512,1024]{1,0:T(8,128)(2,1)S(1)}, f32[256,768]{1,0:T(8,128)S(1)}, bf16[256,256]{1,0:T(8,128)(2,1)S(1)...) custom-call(s32[16]{0:T(128)} %parents_hbm.1, ...), custom_call_target="tpu_custom_call" | custom-call | tf_op jit(solution)/shard_map/transform/pallas_call | solution.py:533
  48.0 2.6 %last.1 = (bf16[768,683]{1,0:T(8,128)(2,1)}, bf16[768,1024]{1,0:T(8,128)(2,1)}) custom-call(bf16[512,683]{1,0:T(8,128)(2,1)S(1)} %get-tuple-element.15.spec_v, bf16[512,1024]{1,0:T(8,128)(2,1)S(1)} %get-tuple-element.16.four_v, f32[256,768]{1,0:T(8,128)S(1)} %get-tuple-element.17.acc, bf16[256,256]{1,0:T(8,128)(2,1)S(1)} %get-tuple-element.18.x, ...), custom_call_target="tpu_custom_call" | custom-call | tf_op jit(solution)/shard_map/last/pallas_call | solution.py:581
